TPU v7x, 512 devices: a whole 4x4x16 slice. The times are simulated.
512 devices in a mesh: dom: 128 (over x, z, core), rep: 4 (over y).
Axes of the slice: x: 4, y: 4, z: 16, core: 2. Of those that a mesh axis runs over, the one named last changes fastest.
Arguments:
- features: float32 [128, 65536], P('rep', 'dom'), may hold values from -6 to 6
- tiles: bfloat16 [5120, 128, 128], P('dom'), may hold values from -0.25 to 0.25
- tile_row: int32 [5120], P('dom'), may hold values from 0 to 3
- tile_col: int32 [5120], P('dom'), may hold values from 0 to 511, as said below
- tile_count: int32 [128], P('dom'), may hold values from 16 to 40, as said below
- dest_slot: int32 [65536], P('dom'), may hold values from 0 to 65535, as said below
- w_in: bfloat16 [128, 1024], replicated, may hold values from -0.5 to 0.5
- w_mid: bfloat16 [1024, 1024], replicated, may hold values from -0.1875 to 0.1875
- w_out: bfloat16 [172, 1024], replicated, may hold values from -0.1875 to 0.1875
- cotangent: bfloat16 [172, 65536], P(None, ('dom', 'rep')), may hold values from -0.0234375 to 0.0234375
Outputs:
- batch_features: float32 [128, 65536], P(None, ('dom', 'rep'))
- grad_w_in: float32 [128, 1024], replicated
- grad_w_mid: float32 [1024, 1024], P('dom')
- grad_w_out: float32 [172, 1024], replicated
Inputs may be any that keep to these rules, and one draw needn't show every extreme that they name: `tile_col`: every slot of partition p, live or not, names a block column within 4 blocks of p's own blocks p * 4 to (p+1) * 4 - 1, counted modulo 512; each of the 8 blocks just before and just after p's own is named by one of p's first 8 slots. `tile_count`: counts vary from partition to partition (several partitions may share a count); at least one partition holds exactly 40 live slots. `dest_slot`: A permutation of the batch positions; each graph partition sends exactly 1 node into each block of 128 consecutive batch positions.
All inputs are finite; a program needn't handle non-finite values.
Results may differ from a plain program's by a relative error of at most 0.006.
Values sent between devices are 32-bit elements; how exact they have to be, the bound alone decides.
A program may use at most 64 MiB of HBM per device.

v0:
```python
import jax
import jax.numpy as jnp
from jax import lax
from jax.sharding import PartitionSpec as P

series_zero = 0.3085083
series_one = -0.4305395
series_two = 0.1864784
LEADING = (((0,), (0,)), ((), ()))
TRAILING = (((1,), (1,)), ((), ()))


def extended_2(cells, sides, width):
    for axis, dim in sides:
        count = lax.axis_size(axis)
        head = lax.slice_in_dim(cells, 0, width, axis=dim)
        tail = lax.slice_in_dim(cells, cells.shape[dim] - width, cells.shape[dim], axis=dim)
        cells = jnp.concatenate(
            [
                lax.ppermute(tail, axis, [(i, (i + 1) % count) for i in range(count)]),
                cells,
                lax.ppermute(head, axis, [((i + 1) % count, i) for i in range(count)]),
            ],
            axis=dim,
        )
    return cells


def silu_slope(pre):
    sigma = jax.nn.sigmoid(pre)
    return sigma * (1.0 + pre * (1.0 - sigma))


def neighbour_blocks(local, margin, tile_size):
    extended = extended_2(local, (("dom", 1),), margin * tile_size)
    return extended


def apply_operator(local, tiles_across, assignment_map, relative, margin):
    feature_count, node_count = local.shape
    tile_size = tiles_across.shape[1]
    extended = neighbour_blocks(local, margin, tile_size)
    blocks = extended.reshape(feature_count, -1, tile_size)
    input_values = jnp.take(blocks, relative, axis=1)
    block_products = jnp.einsum(
        "lkz,glz->glk", tiles_across, input_values, precision=lax.Precision.HIGHEST
    )
    final_result = jnp.einsum(
        "wy,kya->kwa", assignment_map, block_products, precision=lax.Precision.HIGHEST
    )
    return final_result.reshape(feature_count, node_count)


def shards(
    features, tiles, tile_row, tile_col, tile_count, dest_slot, w_in, w_mid, w_out, cotangent
):
    node_partition = lax.axis_index("dom")
    owners = lax.axis_size("dom")
    replicas = lax.axis_size("rep")
    feature_count, node_count = features.shape
    capacity = tiles.shape[0]
    tile_size = tiles.shape[1]
    block_count = node_count // tile_size
    total_blocks = block_count * owners
    relative = jnp.mod(tile_col - node_partition * block_count + block_count, total_blocks)
    live_mask = (jnp.arange(capacity, dtype=jnp.int32) < tile_count[0]).astype(jnp.float32)
    assignment_map = (
        tile_row[None, :] == jnp.arange(block_count, dtype=jnp.int32)[:, None]
    ).astype(jnp.float32) * live_mask[None, :]
    tiles_across = tiles.astype(jnp.float32)
    first = apply_operator(features, tiles_across, assignment_map, relative, block_count)
    second = (
        2.0 * apply_operator(first, tiles_across, assignment_map, relative, block_count) - features
    )
    diffused = series_zero * features + series_one * first + series_two * second
    segment = node_count // (owners * replicas)
    batch_rows = node_count // replicas
    sort_order = jnp.argsort(dest_slot)
    sorted_slots = jnp.take(dest_slot, sort_order)
    moved_rows = jnp.take(diffused, sort_order, axis=1).reshape(
        feature_count, owners, replicas, segment
    )
    moved_slots = sorted_slots.astype(jnp.float32).reshape(1, owners, replicas, segment)
    arrived, arrived_slots = (
        lax.all_to_all(
            lax.all_to_all(moved_rows, "dom", split_axis=1, concat_axis=1, tiled=True),
            "rep",
            split_axis=2,
            concat_axis=0,
            tiled=True,
        ),
        lax.all_to_all(
            lax.all_to_all(moved_slots, "dom", split_axis=1, concat_axis=1, tiled=True),
            "rep",
            split_axis=2,
            concat_axis=0,
            tiled=True,
        ),
    )
    owner_index = node_partition * replicas + lax.axis_index("rep")
    local_slots = arrived_slots[0].reshape(-1).astype(jnp.int32) - owner_index * batch_rows
    gathered = arrived.reshape(feature_count * replicas, -1)
    batch_features = jnp.zeros(gathered.shape, jnp.float32).at[:, local_slots].set(gathered)
    inputs_bf = batch_features.astype(jnp.bfloat16)
    pre_one = lax.dot_general(inputs_bf, w_in, LEADING, preferred_element_type=jnp.float32)
    hidden_one = jax.nn.silu(pre_one).astype(jnp.bfloat16)
    pre_two = jnp.dot(hidden_one, w_mid, preferred_element_type=jnp.float32)
    hidden_two = jax.nn.silu(pre_two).astype(jnp.bfloat16)
    grad_out = jnp.dot(cotangent, hidden_two, preferred_element_type=jnp.float32)
    back_two = lax.dot_general(cotangent, w_out, LEADING, preferred_element_type=jnp.float32)
    delta_two = (back_two * silu_slope(pre_two)).astype(jnp.bfloat16)
    back_one = lax.dot_general(delta_two, w_mid, TRAILING, preferred_element_type=jnp.float32)
    delta_one = (back_one * silu_slope(pre_one)).astype(jnp.bfloat16)
    grad_in = jnp.dot(inputs_bf, delta_one, preferred_element_type=jnp.float32)
    mid_shard = lax.psum_scatter(
        lax.dot_general(hidden_one, delta_two, LEADING, preferred_element_type=jnp.float32),
        "dom",
        scatter_dimension=0,
        tiled=True,
    )
    grad_mid = lax.psum(mid_shard, "rep")
    grad_in, grad_out = lax.psum((grad_in, grad_out), ("dom", "rep"))
    return (batch_features, grad_in, grad_mid, grad_out)


def solution(mesh):
    in_specs = (
        P("rep", "dom"),
        P("dom", None, None),
        P("dom"),
        P("dom"),
        P("dom"),
        P("dom"),
        P(),
        P(),
        P(),
        P(None, ("dom", "rep")),
    )
    out_specs = (P(None, ("dom", "rep")), P(), P("dom", None), P())
    return jax.shard_map(shards, mesh=mesh, in_specs=in_specs, out_specs=out_specs, check_vma=False)
```

profile of v0, /device:TPU:1, one launch (start us, length us, event | category | flops | bytes accessed | tf_op | source)
XLA Modules:
  0.0 604.5 jit_solution(3782618393977635226)
XLA Ops:
  8.0 0.0 copy-start
  8.0 0.0 copy-start.3
  8.0 5.2 collective-permute-start
  13.2 5.8 collective-permute-start.1
  19.0 1.3 compare_and_fusion
  21.0 4.4 sort.17
  25.4 3.6 gather_fusion
  29.1 0.5 compare_convert_fusion
  29.6 1.5 copy_bitcast_fusion
  31.1 2.4 gather_fusion.2
  33.5 3.3 convolution_bitcast_fusion.2
  36.8 0.0 copy-done.6
  36.8 1.5 fusion.6
  38.3 0.6 copy.78
  38.9 1.9 collective-permute-start.2
  40.8 7.7 %collective-permute-start.3 = (f32[32,512]{1,0:T(8,128)}, f32[32,512]{1,0:T(8,128)}, u32[]{:S(2)}, u32[]{:S(2)}) collective-permute-start(f32[32,512]{1,0:T(8,128)} %bitcast.70), channel_id=1, source_target_pairs={{4,0},{8,4},{12,8},{16,12},{20,16},{24,20},{28,24},{32,28},{36,32}... | collective-permute-start | bytes 196616 | tf_op jit(solution)/shard_map/ppermute | solution.py:22
  48.5 0.7 convert_element_type.49
  49.2 14.1 %all-to-all-start = ((f32[1,128,4,1]{2,3,0,1:T(1,128)}), f32[1,128,4,1]{2,3,0,1:T(1,128)}, u32[]{:S(2)}, u32[]{:S(2)}) async-start(f32[1,128,4,1]{2,3,0,1:T(1,128)} %bitcast), calls=%async_computation | async-start | bytes 131072 | tf_op jit(solution)/shard_map/all_to_all | solution.py:93
  63.4 0.1 broadcast_in_dim.39
  63.5 0.9 concatenate.12
  64.4 1.5 concatenate.13
  65.9 0.9 pad_maximum_fusion
  66.7 0.7 copy.59
  67.5 2.5 gather_fusion.3
  70.0 3.3 convolution_bitcast_fusion.1
  73.3 0.0 copy-done.7
  73.3 0.0 copy-start.2
  73.3 0.8 convolution_multiply_fusion.2
  74.2 0.1 copy.61
  74.3 1.2 gather_fusion.1
  75.5 0.2 fusion.47
  75.7 0.8 reshape.166
  76.5 1.3 all-to-all-done
  77.8 14.9 %all-to-all-start.2 = ((f32[128,1,128]{2,1,0:T(1,128)}), f32[128,1,128]{2,1,0:T(1,128)S(1)}, u32[]{:S(2)}, u32[]{:S(2)}) async-start(f32[128,1,128]{2,1,0:T(1,128)} %reshape.166), calls=%async_computation.2 | async-start | bytes 131072 | tf_op jit(solution)/shard_map/all_to_all | solution.py:86
  92.7 1.5 copy.56
  94.2 13.5 %all-to-all-done.2 = f32[128,1,128]{2,1,0:T(1,128)S(1)} async-done(((f32[128,1,128]{2,1,0:T(1,128)}), f32[128,1,128]{2,1,0:T(1,128)S(1)}, u32[]{:S(2)}, u32[]{:S(2)}) %all-to-all-start.2) | async-done | bytes 65568 | tf_op jit(solution)/shard_map/all_to_all | solution.py:86
  107.7 4.2 all-to-all-start.1
  111.9 0.5 broadcast.141
  112.4 0.8 reduce
  113.2 0.2 reshape.167
  113.4 0.7 copy.63
  114.1 1.8 all-to-all-done.1
  115.9 3.3 all-to-all-start.3
  119.2 0.0 reduce-scatter.2.cloned.1.call-start
  119.3 4.4 all-to-all-done.3
  123.7 0.1 copy.64
  123.7 0.9 scatter_custom_fusion
  124.7 0.2 fusion.25
  124.9 0.0 copy-start.10
  124.9 0.5 fusion.46
  125.4 0.5 copy-done.10
  125.9 0.3 fusion
  126.2 2.7 fusion.45
  128.9 0.0 reduce-scatter.2.cloned.1.call-update
  128.9 0.0 all-reduce.3.cloned.1.call-start
  129.0 1.2 convolution_bitcast_fusion
  130.2 1.8 fusion.2
  132.0 0.0 all-reduce.3.cloned.1.call-update
  132.0 0.7 copy.65
  132.8 241.7 %reduce-scatter.2.cloned.1.call-done = f32[8,1024]{1,0:T(8,128)} async-done(((f32[1024,1024]{1,0:T(8,128)}), f32[8,1024]{1,0:T(8,128)}) %reduce-scatter.2.cloned.1.call-update) | async-done | bytes 32784 | tf_op jit(solution)/shard_map/reduce_scatter | solution.py:115
  374.5 15.0 %psum.22 = f32[8,1024]{1,0:T(8,128)} all-reduce(f32[8,1024]{1,0:T(8,128)} %reduce-scatter.2.cloned.1.call-done), channel_id=1, replica_groups=mesh['dom'=128,'rep'=4] {'rep'}, use_global_device_ids=true, to_apply=%region_4.6 | all-reduce | flops 8192 | bytes 65536 | tf_op jit(solution)/shard_map/psum | solution.py:121
  389.4 203.7 %all-reduce.3.cloned.1.call-done = (f32[128,1024]{1,0:T(8,128)}, f32[172,1024]{1,0:T(8,128)}) async-done(((f32[128,1024]{1,0:T(8,128)}, f32[172,1024]{1,0:T(8,128)}), (f32[128,1024]{1,0:T(8,128)}, f32[172,1024]{1,0:T(8,128)})) %all-reduce.3.cloned.1.call-update) | async-done | bytes 1228816 | tf_op jit(solution)/shard_map/psum | solution.py:122
  593.1 1.9 copy.82
  595.0 2.0 copy.83
  (28 shorter events, 0.1 us)
Async XLA Ops:
  8.0 116.9 %copy-start = (bf16[1024,1024]{1,0:T(8,128)(2,1)S(1)}, bf16[1024,1024]{1,0:T(8,128)(2,1)}, u32[]{:S(2)}) copy-start(bf16[1024,1024]{1,0:T(8,128)(2,1)} %param.19) | copy-start | bytes 6291460
  8.0 21.6 %copy-start.3 = (f32[32,512]{1,0:T(8,128)S(1)}, f32[32,512]{1,0:T(8,128)}, u32[]{:S(2)}) copy-start(f32[32,512]{1,0:T(8,128)} %param.12) | copy-start | bytes 196612
  8.0 25.5 %copy-start.1 = (bf16[40,128,128]{2,1,0:T(8,128)(2,1)S(1)}, bf16[40,128,128]{2,1,0:T(8,128)(2,1)}, u32[]{:S(2)}) copy-start(bf16[40,128,128]{2,1,0:T(8,128)(2,1)} %param.13) | copy-start | bytes 3932164
  8.0 21.5 %collective-permute-start = (f32[32,512]{1,0:T(8,128)}, f32[32,512]{1,0:T(8,128)S(1)}, u32[]{:S(2)}, u32[]{:S(2)}) collective-permute-start(f32[32,512]{1,0:T(8,128)} %param.12), channel_id=1, source_target_pairs={{0,4},{4,8},{8,12},{12,16},{16,20},{20,24},{24,28},{28,32},{32,36}... | collective-permute-start | bytes 196616 | tf_op jit(solution)/shard_map/ppermute | solution.py:20
  13.2 16.3 %collective-permute-start.1 = (f32[32,512]{1,0:T(8,128)}, f32[32,512]{1,0:T(8,128)}, u32[]{:S(2)}, u32[]{:S(2)}) collective-permute-start(f32[32,512]{1,0:T(8,128)} %param.12), channel_id=1, source_target_pairs={{4,0},{8,4},{12,8},{16,12},{20,16},{24,20},{28,24},{32,28},{36,32}... | collective-permute-start | bytes 196616 | tf_op jit(solution)/shard_map/ppermute | solution.py:22
  20.3 16.5 %copy-start.6 = (s32[1024]{0:T(1024)}, s32[1024]{0:T(1024)S(1)}, u32[]{:S(2)}) copy-start(s32[1024]{0:T(1024)S(1)} %pad_clamp_fusion) | copy-start | bytes 12292
  25.4 11.3 %copy-start.5 = (s32[1024]{0:T(1024)}, s32[1024]{0:T(1024)S(1)}, u32[]{:S(2)}) copy-start(s32[1024]{0:T(1024)S(1)} %pad_clamp_fusion.1) | copy-start | bytes 12292
  31.1 5.7 copy-start.8
  38.9 24.6 %collective-permute-start.2 = (f32[32,512]{1,0:T(8,128)}, f32[32,512]{1,0:T(8,128)}, u32[]{:S(2)}, u32[]{:S(2)}) collective-permute-start(f32[32,512]{1,0:T(8,128)} %bitcast.70), channel_id=1, source_target_pairs={{0,4},{4,8},{8,12},{12,16},{16,20},{20,24},{24,28},{28,32},{32,36}... | collective-permute-start | bytes 196616 | tf_op jit(solution)/shard_map/ppermute | solution.py:20
  40.8 23.5 %collective-permute-start.3 = (f32[32,512]{1,0:T(8,128)}, f32[32,512]{1,0:T(8,128)}, u32[]{:S(2)}, u32[]{:S(2)}) collective-permute-start(f32[32,512]{1,0:T(8,128)} %bitcast.70), channel_id=1, source_target_pairs={{4,0},{8,4},{12,8},{16,12},{20,16},{24,20},{28,24},{32,28},{36,32}... | collective-permute-start | bytes 196616 | tf_op jit(solution)/shard_map/ppermute | solution.py:22
  49.2 28.6 %all-to-all-start = ((f32[1,128,4,1]{2,3,0,1:T(1,128)}), f32[1,128,4,1]{2,3,0,1:T(1,128)}, u32[]{:S(2)}, u32[]{:S(2)}) async-start(f32[1,128,4,1]{2,3,0,1:T(1,128)} %bitcast), calls=%async_computation | async-start | bytes 131072 | tf_op jit(solution)/shard_map/all_to_all | solution.py:93
  67.5 6.7 %copy-start.4 = (f32[32,512]{1,0:T(8,128)S(1)}, f32[32,512]{1,0:T(8,128)}, u32[]{:S(2)}) copy-start(f32[32,512]{1,0:T(8,128)} %param.12) | copy-start | bytes 196612
  70.0 3.3 copy-start.7
  70.0 3.3 copy-start.9
  73.3 51.3 %copy-start.2 = (bf16[128,1024]{1,0:T(8,128)(2,1)S(1)}, bf16[128,1024]{1,0:T(8,128)(2,1)}, u32[]{:S(2)}) copy-start(bf16[128,1024]{1,0:T(8,128)(2,1)} %param.18) | copy-start | bytes 786436
  77.8 29.9 %all-to-all-start.2 = ((f32[128,1,128]{2,1,0:T(1,128)}), f32[128,1,128]{2,1,0:T(1,128)S(1)}, u32[]{:S(2)}, u32[]{:S(2)}) async-start(f32[128,1,128]{2,1,0:T(1,128)} %reshape.166), calls=%async_computation.2 | async-start | bytes 131072 | tf_op jit(solution)/shard_map/all_to_all | solution.py:86
  107.7 8.2 %all-to-all-start.1 = ((f32[1,128,4,1]{1,3,0,2:T(1,128)}), f32[1,128,4,1]{1,3,0,2:T(1,128)S(1)}, u32[]{:S(2)}, u32[]{:S(2)}) async-start(f32[1,128,4,1]{1,3,0,2:T(1,128)} %copy.56), calls=%async_computation.1 | async-start | bytes 4096 | tf_op jit(solution)/shard_map/all_to_all | solution.py:92
  115.9 7.7 %all-to-all-start.3 = ((f32[32,128,4,1]{1,0,3,2:T(8,128)}), f32[32,128,4,1]{1,0,3,2:T(8,128)S(1)}, u32[]{:S(2)}, u32[]{:S(2)}) async-start(f32[32,128,4,1]{1,0,3,2:T(8,128)} %copy.63), calls=%async_computation.3 | async-start | bytes 131072 | tf_op jit(solution)/shard_map/all_to_all | solution.py:85
  119.2 255.2 %reduce-scatter.2.cloned.1.call-start = ((), (), s32[]{:S(2)}) async-start(), calls=%async_computation.5 | async-start | bytes 4227072 | tf_op jit(solution)/shard_map/reduce_scatter | solution.py:115
  124.9 1.0 copy-start.10
  124.9 1.0 copy-start.11
  128.9 464.2 %all-reduce.3.cloned.1.call-start = ((), (), s32[]{:S(2)}) async-start(), calls=%async_computation.6 | async-start | bytes 2490368 | tf_op jit(solution)/shard_map/psum | solution.py:122
Sparse Core Ops, SparseCore 0:
  129.1 245.3 reduce-scatter.1
Sparse Core Ops, SparseCore 1:
  135.5 457.6 all-reduce.2
where the time goes:
time: 606 us; the launch traced here: 605 us
  waiting for transfers between devices  466 us (77%)
  starting transfers between devices  57.1 us (9%)
  local copies, waits for them, and re-layouts  24.3 us (4%)
  between operations  16.5 us (3%)
  matrix products  15.5 us (3%)
  blocking collectives  15 us (2%)
  other arithmetic  9.71 us (2%)
    reduce_scatter x1, waiting for transfers between devices, shards(): lax.psum_scatter(lax.dot_general(hidden_one, delta_two, LEADING, preferre...  242 us
    psum x1, waiting for transfers between devices, shards(): grad_in, grad_out = lax.psum((grad_in, grad_out), ('dom', 'rep'))  204 us
    psum x1, blocking collectives, shards(): grad_mid = lax.psum(mid_shard, 'rep')  15 us
    all_to_all x1, starting transfers between devices, shards(): lax.all_to_all(moved_rows, 'dom', split_axis=1, concat_axis=1, tiled=True)  14.9 us
    all_to_all x1, starting transfers between devices, shards(): lax.all_to_all(moved_slots, 'dom', split_axis=1, concat_axis=1, tiled=True)  14.1 us
    all_to_all x1, waiting for transfers between devices, shards(): lax.all_to_all(moved_rows, 'dom', split_axis=1, concat_axis=1, tiled=True)  13.5 us
    ppermute x2, starting transfers between devices, extended_2(): lax.ppermute(head, axis, [((i + 1) % count, i) for i in range(count)])  13.4 us
  transfers between devices with their start and end apart: 10, of which 6 were waited for; matrix products, arithmetic and copies ran while one was open for 5% of the time, Pallas kernels for 0%

commit v1 on v0

v1 whole, which is shorter than its diff:
```python
import jax
import jax.numpy as jnp
from jax import lax
from jax.experimental import pallas as pl
from jax.experimental.pallas import tpu as pltpu
from jax.sharding import PartitionSpec as P

series_zero = 0.3085083
series_one = -0.4305395
series_two = 0.1864784
LEADING = (((0,), (0,)), ((), ()))
TRAILING = (((1,), (1,)), ((), ()))
MESH = pl.DeviceIdType.MESH
NX, NY, NZ = 4, 4, 16
F32 = jnp.float32
BF16 = jnp.bfloat16


EX_X, EX_C, EX_B = 0, 1, 2
A_MID, A_IO, B_MID, B_IO = 3, 6, 9, 12
A_TWO, B_TWO = 15, 18
Z_ONE, Z_TWO, Z_ALL = 21, 25, 29
MID_ALL = 53
A_THREE, B_THREE, A_FOUR, B_FOUR, PAIR = 61, 64, 67, 70, 73
HALO_ONE, HALO_TWO = 74, 76
REP_X, Z_X, XC_X = 78, 82, 98
Z_P, XC_P = 106, 122
SEMS = 130


def sigmoid(v):
    return 0.5 + 0.5 * jnp.tanh(0.5 * v)


def split(v):
    high = v.astype(BF16)
    rest = v - high.astype(F32)
    middle = rest.astype(BF16)
    low = (rest - middle.astype(F32)).astype(BF16)
    return high, middle, low


def train_kernel(
    row_hbm, col_hbm, count_hbm, feat_hbm, tiles_hbm, dest_hbm, cot_hbm, w_in_hbm, w_mid_hbm, w_out_hbm,
    out_x, out_in, out_mid, out_out,
    row_ref, col_ref, count_ref, feat, tiles, dest, cot, w_in_ref, w_mid_ref, w_out_ref,
    ext, ext_two, parts, hot, moved, within, amsg, rf, t2, rz2, rx, rq, p2, pz2, px, pq, put,
    x2, cot2, xt, ct, wo, h1, slope1, d2, send_b, recv_b,
    mid, io, ra_mid, ra_io, rb_mid, rb_io, sa, sb, r2a, r2b, zs, rz, zs_two, rz_two, mine, ri, r4, full,
    ssem, rsem, lsem,
):
    loads = []
    for i, (src, dst) in enumerate((
        (feat_hbm, feat), (dest_hbm, dest), (cot_hbm, cot), (row_hbm, row_ref),
        (col_hbm, col_ref), (count_hbm, count_ref), (tiles_hbm, tiles),
        (w_in_hbm, w_in_ref), (w_out_hbm, w_out_ref), (w_mid_hbm, w_mid_ref),
    )):
        loads.append(pltpu.make_async_copy(src, dst, lsem.at[i]))
        loads[-1].start()
    d = lax.axis_index("dom")
    y = lax.axis_index("rep")
    c = d % 2
    z = (d // 2) % NZ
    x = d // (2 * NZ)

    def place(xx, yy, zz, cc):
        return ((xx * NZ + zz) * 2 + cc, yy)

    def copy(src, dst, slot, dev):
        return pltpu.make_async_remote_copy(
            src_ref=src, dst_ref=dst, send_sem=ssem.at[slot], recv_sem=rsem.at[slot],
            device_id=dev, device_id_type=MESH,
        )

    def lanes(index, width):
        return pl.ds(pl.multiple_of(index * width, width), width)

    partner = place(x, y, z, 1 - c)
    far = ((d + 2 * c - 1 + 2 * NX * NZ) % (2 * NX * NZ), y)
    xs = [place((x + k) % NX, y, z, c) for k in range(1, NX)]
    xo = [place((x + k) % NX, y, z, 1 - c) for k in range(1, NX)]
    ys = [place(x, (y + k) % NY, z, c) for k in range(1, NY)]
    yo = [place(x, (y + k) % NY, z, 1 - c) for k in range(1, NY)]
    barrier = pltpu.get_barrier_semaphore()
    for dev in [partner, far] + xs + xo + ys + yo:
        pl.semaphore_signal(barrier, inc=1, device_id=dev, device_id_type=MESH)

    def greet(k, carry):
        pl.semaphore_signal(
            barrier, inc=1, device_id=place(x, y, (z + k) % NZ, c), device_id_type=MESH
        )
        return carry

    lax.fori_loop(1, NZ, greet, 0)

    for one in loads[:3]:
        one.wait()
    own = jnp.stack([feat[:, pl.ds(128 * b, 128)] for b in range(4)])
    ext[4:8] = own
    for i, part in enumerate(split(own)):
        parts[4:8, pl.ds(32 * i, 32)] = part
    cot2[c] = jnp.zeros((192, 128), F32)
    cot2[c, 0:172] = cot[...].astype(F32)
    pl.semaphore_wait(barrier, 2 + 3 + 3 + 3 + 3 + NZ - 1)

    def halo(field, slot):
        one = copy(field.at[pl.ds(4, 4)], field.at[pl.ds(8 * c, 4)], slot, partner)
        two = copy(field.at[pl.ds(4, 4)], field.at[pl.ds(8 * (1 - c), 4)], slot + 1, far)
        two.start()
        one.start()
        return one, two

    near, wide = halo(ext, HALO_ONE)
    ex_c = copy(cot2.at[c], cot2.at[c], EX_C, partner)
    ex_c.start()
    copies = [near, wide, ex_c]

    j = lax.broadcasted_iota(jnp.int32, (512, 128), 0)
    target = ((((j >> 1) & 3) * NZ + ((j >> 3) & 15)) * 2 + (j & 1)) * NY + (j >> 7)
    for b in range(4):
        line = dest[pl.ds(b, 1), :]
        hot[:, pl.ds(128 * b, 128)] = jnp.where(target == (line >> 7), 1.0, 0.0).astype(BF16)
        within[:, pl.ds(128 * b, 128)] = jnp.broadcast_to(
            (line & 127).astype(F32), (128, 128)
        ).astype(BF16)

    p2[...] = lax.dot_general(
        hot[lanes(y, 128), :], within[...], TRAILING, preferred_element_type=F32
    ).reshape(NZ, 8, 128)
    mine_xc = x * 2 + c

    def over_z(src, dst, slot):
        def one(k):
            to = (z + k) % NZ
            return copy(src.at[to], dst.at[z], slot + k, place(x, y, to, c))

        def start(k, carry):
            one(k).start()
            return carry

        def recv(k, carry):
            one(k).wait_recv()
            return carry

        def sent(k, carry):
            one(k).wait_send()
            return carry

        return start, recv, sent

    def over_xc(src, dst, slot):
        made = []
        for k in (2, 1, 3, 0):
            to = (x + k) % NX
            if k:
                made.append(copy(src.at[to * 2 + c], dst.at[mine_xc], slot + k, xs[k - 1]))
                made[-1].start()
            dev = xo[k - 1] if k else partner
            made.append(copy(src.at[to * 2 + 1 - c], dst.at[mine_xc], slot + 4 + k, dev))
            made[-1].start()
        return made

    pz_start, pz_recv, pz_sent = over_z(p2, pz2, Z_P)
    lax.fori_loop(1, NZ, pz_start, 0)
    pz2[z] = p2[z]
    wo[...] = jnp.zeros((192, 1024), BF16)
    for one in loads[3:]:
        one.wait()
    wo[0:172, :] = w_out_ref[...]

    count = count_ref[0]

    def spread(field, near, wide):
        near.wait_recv()
        for i, part in enumerate(split(field[pl.ds(8 * (1 - c), 4)])):
            parts[pl.ds(8 * (1 - c), 4), pl.ds(32 * i, 32)] = part
        wide.wait_recv()
        for i, part in enumerate(split(field[pl.ds(8 * c, 4)])):
            parts[pl.ds(8 * c, 4), pl.ds(32 * i, 32)] = part

        def slots(i, sums):
            for u in range(5):
                s = i * 5 + u
                at = jnp.minimum((col_ref[s] - 4 * d + 4) & 511, 11)
                product = lax.dot_general(
                    parts[at], tiles[s], TRAILING, preferred_element_type=F32
                )
                total = product[0:32] + product[32:64] + product[64:96]
                row = jnp.where(s < count, row_ref[s], -1)
                sums = tuple(
                    v + jnp.where(row == b, 1.0, 0.0) * total for b, v in enumerate(sums)
                )
            return sums

        zero = jnp.zeros((32, 128), F32)
        return jnp.stack(lax.fori_loop(0, 8, slots, (zero,) * 4))

    first = spread(ext, near, wide)
    ext_two[4:8] = first
    near, wide = halo(ext_two, HALO_TWO)
    copies += [near, wide]
    for i, part in enumerate(split(first)):
        parts[4:8, pl.ds(32 * i, 32)] = part
    lax.fori_loop(1, NZ, pz_recv, 0)
    for i in range(8):
        px[i] = pz2[:, i, :]
    xc_p = over_xc(px, pq, XC_P)
    pq[mine_xc] = px[mine_xc]
    copies += xc_p
    second = spread(ext_two, near, wide)
    second = 2.0 * second - ext[4:8]
    diffused = series_zero * ext[4:8] + series_one * ext_two[4:8] + series_two * second

    for i, part in enumerate(split(diffused)):
        for b in range(4):
            moved[pl.ds(32 * i, 32), pl.ds(128 * b, 128)] = part[b]
    sorted_rows = lax.dot_general(moved[...], hot[...], TRAILING, preferred_element_type=F32)
    columns = sorted_rows[0:32] + sorted_rows[32:64] + sorted_rows[64:96]
    for i in range(NY):
        amsg[i] = columns[:, 128 * i : 128 * i + 128]
    rep_x = []
    for k in (2, 1, 3):
        to = (y + k) % NY
        rep_x.append(copy(amsg.at[to], rf.at[y], REP_X + k, ys[k - 1]))
        rep_x[-1].start()
    rf[y] = amsg[y]
    for one in xc_p:
        one.wait_recv()
    at_lane = lax.broadcasted_iota(jnp.int32, (128, 128), 1).astype(F32)
    put[...] = jnp.where(pq[...].reshape(128, 128) == at_lane, 1.0, 0.0).astype(BF16)
    for one in rep_x:
        one.wait_recv()
    t2[...] = rf[...].reshape(128, 128).T.reshape(NZ, 8, 128)
    zx_start, zx_recv, zx_sent = over_z(t2, rz2, Z_X)
    lax.fori_loop(1, NZ, zx_start, 0)
    rz2[z] = t2[z]
    lax.fori_loop(1, NZ, zx_recv, 0)
    for i in range(8):
        rx[i] = rz2[:, i, :]
    xc_x = over_xc(rx, rq, XC_X)
    rq[mine_xc] = rx[mine_xc]
    for one in xc_x:
        one.wait_recv()
    copies += rep_x + xc_x
    lines = jnp.concatenate(split(rq[...].reshape(128, 128).T), axis=0)
    placed = jnp.dot(lines, put[...], preferred_element_type=F32)
    batch = placed[0:128] + placed[128:256] + placed[256:384]
    out_x[...] = batch

    x2[c] = batch
    ex_x = copy(x2.at[c], x2.at[c], EX_X, partner)
    ex_x.start()
    ex_c.wait_recv()
    for i in range(2):
        ct[pl.ds(128 * i, 128), :] = cot2[i].T.astype(BF16)
    ex_x.wait_recv()
    for i in range(2):
        xt[pl.ds(128 * i, 128), :] = x2[i].T.astype(BF16)

    for j in range(4):
        cols = pl.ds(256 * j, 256)
        pre = jnp.dot(xt[...], w_in_ref[:, cols], preferred_element_type=F32)
        g = sigmoid(pre)
        h1[:, cols] = (pre * g).astype(BF16)
        slope1[j] = g * (1.0 + pre * (1.0 - g))
    half = lanes(c, 512)
    pre_two = jnp.dot(h1[...], w_mid_ref[:, half], preferred_element_type=F32)
    g_two = sigmoid(pre_two)
    h2 = (pre_two * g_two).astype(BF16)
    back_two = jnp.dot(ct[...], wo[:, half], preferred_element_type=F32)
    d2[...] = (back_two * (g_two * (1.0 + pre_two * (1.0 - g_two)))).astype(BF16)

    send_b[...] = lax.dot_general(
        d2[...], w_mid_ref[lanes(1 - c, 512), half], TRAILING, preferred_element_type=F32
    )
    ex_b = copy(send_b, recv_b, EX_B, partner)
    ex_b.start()

    copies += [ex_x, ex_b]
    first_a = []
    for k in (2, 1, 3, 0):
        to = (x + k) % NX
        rows = lax.dot_general(
            h1[:, lanes(to, 256)], d2[...], LEADING, preferred_element_type=F32
        ).reshape(NZ, 2, 8, 512)
        mid[0, to] = rows[:, 0]
        mid[1, to] = rows[:, 1]
        if k:
            one = copy(mid.at[0, to], ra_mid.at[k - 1], A_MID + k - 1, xs[k - 1])
            one.start()
            first_a.append(one)
    first_b = []
    for k in (2, 1, 3):
        one = copy(
            mid.at[1, :, :, :, lanes((y + k) % NY, 128)], rb_mid.at[k - 1], B_MID + k - 1, ys[k - 1]
        )
        one.start()
        first_b.append(one)

    cot_rows = [cot2[i].astype(BF16) for i in range(2)]
    grad_out = jnp.dot(
        jnp.concatenate(cot_rows, axis=1), h2, preferred_element_type=F32
    ).reshape(24, 8, 512)
    own_back = lax.dot_general(
        d2[...], w_mid_ref[half, half], TRAILING, preferred_element_type=F32
    )
    ex_b.wait_recv()
    slope = jnp.concatenate([slope1[2 * c], slope1[2 * c + 1]], axis=1)
    delta_one = ((own_back + recv_b[...]) * slope).astype(BF16)
    x_rows = jnp.concatenate([x2[i].astype(BF16) for i in range(2)], axis=1)
    grad_in = jnp.dot(x_rows, delta_one, preferred_element_type=F32).reshape(16, 8, 512)
    io[0:16] = grad_in
    io[16:40] = grad_out
    for k in (2, 1, 3):
        to = (x + k) % NX
        one = copy(io.at[pl.ds(to * 5, 5)], ra_io.at[k - 1], A_IO + k - 1, xs[k - 1])
        one.start()
        first_a.append(one)
        one = copy(
            io.at[pl.ds(20, 20), :, lanes((y + k) % NY, 128)], rb_io.at[k - 1], B_IO + k - 1, ys[k - 1]
        )
        one.start()
        first_b.append(one)
    copies += first_a + first_b

    y_lane = lanes(y, 128)
    for one in first_a:
        one.wait_recv()
    sa[0:16] = mid[0, x] + ra_mid[0] + ra_mid[1] + ra_mid[2]
    sa[16:21] = io[pl.ds(x * 5, 5)] + ra_io[0] + ra_io[1] + ra_io[2]
    second = []
    for k in (2, 1, 3):
        one = copy(
            sa.at[:, :, lanes((y + k) % NY, 128)], r2a.at[k - 1], A_TWO + k - 1, ys[k - 1]
        )
        one.start()
        second.append(one)
    for one in first_b:
        one.wait_recv()
    for i in range(NX):
        sb[i, 0:16] = mid[1, i, :, :, y_lane] + rb_mid[0, i] + rb_mid[1, i] + rb_mid[2, i]
        at = pl.ds(5 * i, 5)
        sb[i, 16:21] = io[pl.ds(20 + 5 * i, 5), :, y_lane] + rb_io[0, at] + rb_io[1, at] + rb_io[2, at]
    for k in (2, 1, 3):
        one = copy(sb.at[(x + k) % NX], r2b.at[k - 1], B_TWO + k - 1, xs[k - 1])
        one.start()
        second.append(one)
    for one in second:
        one.wait_recv()
    copies += second
    sum_a = sa[:, :, y_lane] + r2a[0] + r2a[1] + r2a[2]
    sum_b = sb[x] + r2b[0] + r2b[1] + r2b[2]

    group, spot_z = z // 4, z % 4
    io_tiles = [sum_a[16 + t] for t in range(5)] + [sum_b[16 + t] for t in range(5)]
    io_tiles += [jnp.zeros((8, 128), F32)] * 2
    for i in range(4):
        for g in range(4):
            zs[i, g] = sum_a[4 * g + i]
            zs[i, 4 + g] = sum_b[4 * g + i]
        for t in range(3):
            zs[i, 8 + t] = io_tiles[4 * t + i]
    third = []
    for k in (2, 1, 3):
        to = (spot_z + k) % 4
        third.append(
            copy(zs.at[to], rz.at[k - 1], Z_ONE + k, place(x, y, group * 4 + to, c))
        )
        third[-1].start()
    for one in third:
        one.wait_recv()
    grouped = zs[spot_z] + rz[0] + rz[1] + rz[2]
    for g in range(4):
        zs_two[g, 0] = grouped[g]
        zs_two[g, 1] = grouped[4 + g]
        zs_two[g, 2:5] = grouped[8:11]
    across = []
    for k in (2, 1, 3):
        to = (group + k) % 4
        across.append(
            copy(zs_two.at[to], rz_two.at[group], Z_TWO + k, place(x, y, to * 4 + spot_z, c))
        )
        across[-1].start()
    rz_two[group] = zs_two[group]
    for one in across:
        one.wait_recv()
    copies += third + across
    mine[...] = ((rz_two[0] + rz_two[1]) + rz_two[2]) + rz_two[3]

    last = []
    for k in range(NY):
        if k:
            one = copy(mine.at[c], r4.at[c, y], MID_ALL + k, ys[k - 1])
            one.start()
            last.append(one)
        one = copy(
            mine.at[1 - c], r4.at[c, y], MID_ALL + 4 + k, yo[k - 1] if k else partner
        )
        one.start()
        last.append(one)
    r4[c, y] = mine[c]
    copies += last

    share = []
    for k in (2, 1, 3):
        share.append(
            copy(
                mine.at[pl.ds(2, 3)], ri.at[spot_z], Z_ALL + k,
                place(x, y, group * 4 + (spot_z + k) % 4, c),
            )
        )
        share[-1].start()
    ri[spot_z] = mine[2:5]
    for one in share:
        one.wait_recv()
    copies += share
    tile = lanes(c * NY + y, 128)
    rows_a, rows_b = pl.ds(x * 5, 5), pl.ds((NX + x) * 5, 5)
    for t in range(10):
        full[(t // 5 * NX + x) * 5 + t % 5, :, tile] = ri[t % 4, t // 4]
    third = []
    for k in (2, 1, 3):
        spot = full.at[rows_a, :, tile]
        third.append(copy(spot, spot, A_THREE + k - 1, ys[k - 1]))
        third[-1].start()
        spot = full.at[rows_b, :, tile]
        third.append(copy(spot, spot, B_THREE + k - 1, xs[k - 1]))
        third[-1].start()
    for one in third:
        one.wait_recv()
    fourth = []
    for k in (2, 1, 3):
        spot = full.at[rows_a, :, half]
        fourth.append(copy(spot, spot, A_FOUR + k - 1, xs[k - 1]))
        fourth[-1].start()
        spot = full.at[pl.ds(20, 20), :, tile]
        fourth.append(copy(spot, spot, B_FOUR + k - 1, ys[k - 1]))
        fourth[-1].start()
    for one in fourth:
        one.wait_recv()
    spot = full.at[:, :, half]
    pair = copy(spot, spot, PAIR, partner)
    pair.start()
    for one in last:
        one.wait_recv()
    for i in range(8):
        out_mid[:, pl.ds(128 * i, 128)] = r4[i // 4, i % 4]
    copies += third + fourth + [pair]
    pair.wait_recv()
    out_in[...] = full[0:16].reshape(128, 1024)
    out_out[...] = full[16:40].reshape(192, 1024)[0:172]

    lax.fori_loop(1, NZ, pz_sent, 0)
    lax.fori_loop(1, NZ, zx_sent, 0)
    for one in copies:
        one.wait_send()


def train(tile_row, tile_col, tile_count, features, tiles, dest, cotangent, w_in, w_mid, w_out):
    vmem = pl.BlockSpec(memory_space=pltpu.VMEM)
    hbm = pl.BlockSpec(memory_space=pltpu.HBM)
    buf = pltpu.VMEM
    return pl.pallas_call(
        train_kernel,
        out_shape=(
            jax.ShapeDtypeStruct((128, 128), F32),
            jax.ShapeDtypeStruct((128, 1024), F32),
            jax.ShapeDtypeStruct((8, 1024), F32),
            jax.ShapeDtypeStruct((172, 1024), F32),
        ),
        in_specs=[hbm] * 10,
        out_specs=(vmem,) * 4,
        scratch_shapes=[
            pltpu.SMEM((40,), jnp.int32),
            pltpu.SMEM((40,), jnp.int32),
            pltpu.SMEM((1,), jnp.int32),
            buf((32, 512), F32),
            buf((40, 128, 128), BF16),
            buf((4, 128), jnp.int32),
            buf((172, 128), BF16),
            buf((128, 1024), BF16),
            buf((1024, 1024), BF16),
            buf((172, 1024), BF16),
            buf((12, 32, 128), F32),
            buf((12, 32, 128), F32),
            buf((12, 96, 128), BF16),
            buf((512, 512), BF16),
            buf((96, 512), BF16),
            buf((128, 512), BF16),
            buf((NY, 32, 128), F32),
            buf((NY, 32, 128), F32),
            buf((NZ, 8, 128), F32),
            buf((NZ, 8, 128), F32),
            buf((8, NZ, 128), F32),
            buf((8, NZ, 128), F32),
            buf((NZ, 8, 128), F32),
            buf((NZ, 8, 128), F32),
            buf((8, NZ, 128), F32),
            buf((8, NZ, 128), F32),
            buf((128, 128), BF16),
            buf((2, 128, 128), F32),
            buf((2, 192, 128), F32),
            buf((256, 128), BF16),
            buf((256, 192), BF16),
            buf((192, 1024), BF16),
            buf((256, 1024), BF16),
            buf((4, 256, 256), F32),
            buf((256, 512), BF16),
            buf((256, 512), F32),
            buf((256, 512), F32),
            buf((2, NX, NZ, 8, 512), F32),
            buf((40, 8, 512), F32),
            buf((3, NZ, 8, 512), F32),
            buf((3, 5, 8, 512), F32),
            buf((3, NX, NZ, 8, 128), F32),
            buf((3, 20, 8, 128), F32),
            buf((21, 8, 512), F32),
            buf((NX, 21, 8, 128), F32),
            buf((3, 21, 8, 128), F32),
            buf((3, 21, 8, 128), F32),
            buf((4, 11, 8, 128), F32),
            buf((3, 11, 8, 128), F32),
            buf((4, 5, 8, 128), F32),
            buf((4, 5, 8, 128), F32),
            buf((5, 8, 128), F32),
            buf((4, 3, 8, 128), F32),
            buf((2, NY, 8, 128), F32),
            buf((40, 8, 1024), F32),
            pltpu.SemaphoreType.DMA((SEMS,)),
            pltpu.SemaphoreType.DMA((SEMS,)),
            pltpu.SemaphoreType.DMA((10,)),
        ],
        compiler_params=pltpu.CompilerParams(
            collective_id=0, has_side_effects=True, vmem_limit_bytes=60 * 1024 * 1024
        ),
    )(tile_row, tile_col, tile_count, features, tiles, dest, cotangent, w_in, w_mid, w_out)


def shards(
    features, tiles, tile_row, tile_col, tile_count, dest_slot, w_in, w_mid, w_out, cotangent
):
    dest = dest_slot.reshape(4, 128)
    return train(
        tile_row, tile_col, tile_count, features, tiles, dest, cotangent, w_in, w_mid, w_out
    )


def solution(mesh):
    in_specs = (
        P("rep", "dom"),
        P("dom", None, None),
        P("dom"),
        P("dom"),
        P("dom"),
        P("dom"),
        P(),
        P(),
        P(),
        P(None, ("dom", "rep")),
    )
    out_specs = (P(None, ("dom", "rep")), P(), P("dom", None), P())
    return jax.shard_map(shards, mesh=mesh, in_specs=in_specs, out_specs=out_specs, check_vma=False)
```

time: 606 us -> 113 us (0.19)
  waiting for transfers between devices: 466 us -> 0 us
  Pallas kernels: 0 us -> 105 us
  starting transfers between devices: 57.1 us -> 0 us
  local copies, waits for them, and re-layouts: 24.3 us -> 6.77 us
  matrix products: 15.5 us -> 0 us
  between operations: 16.5 us -> 1.29 us
  blocking collectives: 15 us -> 0 us
  other arithmetic: 9.71 us -> 0 us
    reduce_scatter x1 -> x0, waiting for transfers between devices: 242 us -> none  [shards(): lax.psum_scatter(lax.dot_general(hidden_one, delta_two, LEADING, preferre...]
    psum x1 -> x0, waiting for transfers between devices: 204 us -> none  [shards(): grad_in, grad_out = lax.psum((grad_in, grad_out), ('dom', 'rep'))]
    pallas_call x0 -> x1, Pallas kernels: none -> 105 us  [train(): pl.pallas_call(train_kernel, out_shape=(jax.ShapeDtypeStruct((128, 128),...]
    all_to_all x4 -> x0, starting transfers between devices: 36.5 us -> none  [the longest x1 14.9 us: shards(): lax.all_to_all(moved_rows, 'dom', split_axis=1, concat_axis=1, tiled=True)]
    all_to_all x4 -> x0, waiting for transfers between devices: 21 us -> none  [the longest x1 13.5 us: shards(): lax.all_to_all(moved_rows, 'dom', split_axis=1, concat_axis=1, tiled=True)]
    ppermute x4 -> x0, starting transfers between devices: 20.6 us -> none  [the longest x2 13.4 us: extended_2(): lax.ppermute(head, axis, [((i + 1) % count, i) for i in range(count)])]
    dot_general x10 -> x0, matrix products: 15.5 us -> none  [the longest x2 6.55 us: apply_operator(): jnp.einsum('lkz,glz->glk', tiles_across, input_values, precision=lax.Prec...]
    psum x1 -> x0, blocking collectives: 15 us -> none  [shards(): grad_mid = lax.psum(mid_shard, 'rep')]
  transfers between devices with their start and end apart: 10 -> 0, of which waited for: 6 -> 0; matrix products, arithmetic and copies ran while one was open for 5% -> 0% of each run, Pallas kernels for 0% -> 0%
where the time goes in v1:
time: 113 us
  Pallas kernels  105 us (93%)
  local copies, waits for them, and re-layouts  6.77 us (6%)
  between operations  1.29 us (1%)
    pallas_call x1, Pallas kernels, train(): pl.pallas_call(train_kernel, out_shape=(jax.ShapeDtypeStruct((128, 128),...  105 us
    unnamed x4, local copies, waits for them, and re-layouts  6.77 us

profile of v1, /device:TPU:1, one launch (start us, length us, event | category | flops | bytes accessed | tf_op | source)
XLA Modules:
  0.0 112.7 jit_solution(6006543283380018839)
XLA Ops:
  1.3 104.7 %shard_map.129 = (f32[128,128]{1,0:T(8,128)}, f32[128,1024]{1,0:T(8,128)}, f32[8,1024]{1,0:T(8,128)}, f32[172,1024]{1,0:T(8,128)}) custom-call(s32[40]{0:T(128)} %row_hbm.1, s32[40]{0:T(128)} %col_hbm.1, s32[1]{0:T(128)S(6)} %copy.18.count_hbm, f32[32,512]{1,0:T(8,128)} %feat_hbm.1, bf16[40,128,128]{2,1,0:T(8,128)(2,1)} %tiles_hbm.1, s32[4,128]{1,0:T(4,128)} %bitcast.1, ...), custom_call_target="tpu_custom_call" | custom-call | tf_op jit(solution)/shard_map/pallas_call | solution.py:463
  106.0 1.5 %copy.19 = f32[128,128]{1,0:T(8,128)} copy(f32[128,128]{1,0:T(8,128)} %get-tuple-element.8) | data formatting | bytes 131072
  107.4 1.9 %copy.20 = f32[128,1024]{1,0:T(8,128)} copy(f32[128,1024]{1,0:T(8,128)} %get-tuple-element.9) | data formatting | bytes 1048576
  109.3 1.4 %copy.21 = f32[8,1024]{1,0:T(8,128)} copy(f32[8,1024]{1,0:T(8,128)} %get-tuple-element.10) | data formatting | bytes 65536
  110.7 2.0 %copy.22 = f32[172,1024]{1,0:T(8,128)} copy(f32[172,1024]{1,0:T(8,128)} %get-tuple-element.11) | data formatting | bytes 1409024

commit v2 on v1

--- a/solution.py
+++ b/solution.py
@@ -25,7 +25,8 @@
 HALO_ONE, HALO_TWO = 74, 76
 REP_X, Z_X, XC_X = 78, 82, 98
 Z_P, XC_P = 106, 122
-SEMS = 130
+A_TWO_IO, B_TWO_IO, Z_ONE_IO, Z_TWO_IO = 130, 133, 136, 140
+SEMS = 144
 
 
 def sigmoid(v):
@@ -41,18 +42,19 @@
 
 
 def train_kernel(
-    row_hbm, col_hbm, count_hbm, feat_hbm, tiles_hbm, dest_hbm, cot_hbm, w_in_hbm, w_mid_hbm, w_out_hbm,
+    count_ref, row_hbm, col_hbm, feat_hbm, tiles_hbm, dest_hbm, cot_hbm, w_in_hbm, w_mid_hbm, w_out_hbm,
     out_x, out_in, out_mid, out_out,
-    row_ref, col_ref, count_ref, feat, tiles, dest, cot, w_in_ref, w_mid_ref, w_out_ref,
+    row_ref, col_ref, feat, tiles, dest, cot, w_in_ref, w_mid_ref, w_out_ref,
     ext, ext_two, parts, hot, moved, within, amsg, rf, t2, rz2, rx, rq, p2, pz2, px, pq, put,
     x2, cot2, xt, ct, wo, h1, slope1, d2, send_b, recv_b,
     mid, io, ra_mid, ra_io, rb_mid, rb_io, sa, sb, r2a, r2b, zs, rz, zs_two, rz_two, mine, ri, r4, full,
+    sai, sbi, r2ai, r2bi, zi, rzi, rzi_two, mine_io,
     ssem, rsem, lsem,
 ):
     loads = []
     for i, (src, dst) in enumerate((
         (feat_hbm, feat), (dest_hbm, dest), (cot_hbm, cot), (row_hbm, row_ref),
-        (col_hbm, col_ref), (count_hbm, count_ref), (tiles_hbm, tiles),
+        (col_hbm, col_ref), (tiles_hbm, tiles),
         (w_in_hbm, w_in_ref), (w_out_hbm, w_out_ref), (w_mid_hbm, w_mid_ref),
     )):
         loads.append(pltpu.make_async_copy(src, dst, lsem.at[i]))
@@ -101,20 +103,6 @@
         parts[4:8, pl.ds(32 * i, 32)] = part
     cot2[c] = jnp.zeros((192, 128), F32)
     cot2[c, 0:172] = cot[...].astype(F32)
-    pl.semaphore_wait(barrier, 2 + 3 + 3 + 3 + 3 + NZ - 1)
-
-    def halo(field, slot):
-        one = copy(field.at[pl.ds(4, 4)], field.at[pl.ds(8 * c, 4)], slot, partner)
-        two = copy(field.at[pl.ds(4, 4)], field.at[pl.ds(8 * (1 - c), 4)], slot + 1, far)
-        two.start()
-        one.start()
-        return one, two
-
-    near, wide = halo(ext, HALO_ONE)
-    ex_c = copy(cot2.at[c], cot2.at[c], EX_C, partner)
-    ex_c.start()
-    copies = [near, wide, ex_c]
-
     j = lax.broadcasted_iota(jnp.int32, (512, 128), 0)
     target = ((((j >> 1) & 3) * NZ + ((j >> 3) & 15)) * 2 + (j & 1)) * NY + (j >> 7)
     for b in range(4):
@@ -127,6 +115,19 @@
     p2[...] = lax.dot_general(
         hot[lanes(y, 128), :], within[...], TRAILING, preferred_element_type=F32
     ).reshape(NZ, 8, 128)
+    pl.semaphore_wait(barrier, 2 + 3 + 3 + 3 + 3 + NZ - 1)
+
+    def halo(field, slot):
+        one = copy(field.at[pl.ds(4, 4)], field.at[pl.ds(8 * c, 4)], slot, partner)
+        two = copy(field.at[pl.ds(4, 4)], field.at[pl.ds(8 * (1 - c), 4)], slot + 1, far)
+        two.start()
+        one.start()
+        return one, two
+
+    near, wide = halo(ext, HALO_ONE)
+    ex_c = copy(cot2.at[c], cot2.at[c], EX_C, partner)
+    ex_c.start()
+    copies = [near, wide, ex_c]
     mine_xc = x * 2 + c
 
     def over_z(src, dst, slot):
@@ -277,30 +278,11 @@
     ex_b.start()
 
     copies += [ex_x, ex_b]
-    first_a = []
-    for k in (2, 1, 3, 0):
-        to = (x + k) % NX
-        rows = lax.dot_general(
-            h1[:, lanes(to, 256)], d2[...], LEADING, preferred_element_type=F32
-        ).reshape(NZ, 2, 8, 512)
-        mid[0, to] = rows[:, 0]
-        mid[1, to] = rows[:, 1]
-        if k:
-            one = copy(mid.at[0, to], ra_mid.at[k - 1], A_MID + k - 1, xs[k - 1])
-            one.start()
-            first_a.append(one)
-    first_b = []
-    for k in (2, 1, 3):
-        one = copy(
-            mid.at[1, :, :, :, lanes((y + k) % NY, 128)], rb_mid.at[k - 1], B_MID + k - 1, ys[k - 1]
-        )
-        one.start()
-        first_b.append(one)
-
     cot_rows = [cot2[i].astype(BF16) for i in range(2)]
     grad_out = jnp.dot(
         jnp.concatenate(cot_rows, axis=1), h2, preferred_element_type=F32
     ).reshape(24, 8, 512)
+    io[16:40] = grad_out
     own_back = lax.dot_general(
         d2[...], w_mid_ref[half, half], TRAILING, preferred_element_type=F32
     )
@@ -310,145 +292,169 @@
     x_rows = jnp.concatenate([x2[i].astype(BF16) for i in range(2)], axis=1)
     grad_in = jnp.dot(x_rows, delta_one, preferred_element_type=F32).reshape(16, 8, 512)
     io[0:16] = grad_in
-    io[16:40] = grad_out
-    for k in (2, 1, 3):
+
+    def send(src, dst, slot, dev):
+        one = copy(src, dst, slot, dev)
+        one.start()
+        copies.append(one)
+        return one
+
+    def arrive(made):
+        for one in made:
+            one.wait_recv()
+
+    first_a, first_b = [], []
+    for k in (2, 1, 3):
+        first_a.append(
+            send(io.at[pl.ds((x + k) % NX * 5, 5)], ra_io.at[k - 1], A_IO + k - 1, xs[k - 1])
+        )
+        first_b.append(
+            send(
+                io.at[pl.ds(20, 20), :, lanes((y + k) % NY, 128)],
+                rb_io.at[k - 1], B_IO + k - 1, ys[k - 1],
+            )
+        )
+
+    mid_a, mid_b = [], []
+    for k in (2, 1, 3, 0):
         to = (x + k) % NX
-        one = copy(io.at[pl.ds(to * 5, 5)], ra_io.at[k - 1], A_IO + k - 1, xs[k - 1])
-        one.start()
-        first_a.append(one)
-        one = copy(
-            io.at[pl.ds(20, 20), :, lanes((y + k) % NY, 128)], rb_io.at[k - 1], B_IO + k - 1, ys[k - 1]
-        )
-        one.start()
-        first_b.append(one)
-    copies += first_a + first_b
+        rows = lax.dot_general(
+            h1[:, lanes(to, 256)], d2[...], LEADING, preferred_element_type=F32
+        ).reshape(NZ, 2, 8, 512)
+        mid[0, to] = rows[:, 0]
+        mid[1, to] = rows[:, 1]
+        if k:
+            mid_a.append(send(mid.at[0, to], ra_mid.at[k - 1], A_MID + k - 1, xs[k - 1]))
+    for k in (2, 1, 3):
+        mid_b.append(
+            send(
+                mid.at[1, :, :, :, lanes((y + k) % NY, 128)],
+                rb_mid.at[k - 1], B_MID + k - 1, ys[k - 1],
+            )
+        )
 
     y_lane = lanes(y, 128)
-    for one in first_a:
-        one.wait_recv()
-    sa[0:16] = mid[0, x] + ra_mid[0] + ra_mid[1] + ra_mid[2]
-    sa[16:21] = io[pl.ds(x * 5, 5)] + ra_io[0] + ra_io[1] + ra_io[2]
-    second = []
-    for k in (2, 1, 3):
-        one = copy(
-            sa.at[:, :, lanes((y + k) % NY, 128)], r2a.at[k - 1], A_TWO + k - 1, ys[k - 1]
-        )
-        one.start()
-        second.append(one)
-    for one in first_b:
-        one.wait_recv()
+    two_io = []
+    arrive(first_a)
+    sai[...] = io[pl.ds(x * 5, 5)] + ra_io[0] + ra_io[1] + ra_io[2]
+    for k in (2, 1, 3):
+        two_io.append(
+            send(sai.at[:, :, lanes((y + k) % NY, 128)], r2ai.at[k - 1], A_TWO_IO + k - 1, ys[k - 1])
+        )
+    arrive(first_b)
+    sbi[...] = io[20:40, :, y_lane] + rb_io[0] + rb_io[1] + rb_io[2]
+    for k in (2, 1, 3):
+        two_io.append(
+            send(sbi.at[pl.ds((x + k) % NX * 5, 5)], r2bi.at[k - 1], B_TWO_IO + k - 1, xs[k - 1])
+        )
+    arrive(two_io)
+    io_a = sai[:, :, y_lane] + r2ai[0] + r2ai[1] + r2ai[2]
+    io_b = sbi[pl.ds(x * 5, 5)] + r2bi[0] + r2bi[1] + r2bi[2]
+
+    group, spot_z = z // 4, z % 4
+    tiles_io = [io_a[t] for t in range(5)] + [io_b[t] for t in range(5)]
+    tiles_io += [jnp.zeros((8, 128), F32)] * 2
+    for i in range(4):
+        for t in range(3):
+            zi[i, t] = tiles_io[4 * t + i]
+    near_z = [place(x, y, group * 4 + (spot_z + k) % 4, c) for k in range(1, 4)]
+    far_z = [place(x, y, (z + 4 * k) % NZ, c) for k in range(1, 4)]
+    third_io = []
+    for k in (2, 1, 3):
+        third_io.append(
+            send(zi.at[(spot_z + k) % 4], rzi.at[k - 1], Z_ONE_IO + k, near_z[k - 1])
+        )
+    arrive(third_io)
+    rzi_two[group] = zi[spot_z] + rzi[0] + rzi[1] + rzi[2]
+    across_io = []
+    for k in (2, 1, 3):
+        across_io.append(
+            send(rzi_two.at[group], rzi_two.at[group], Z_TWO_IO + k, far_z[k - 1])
+        )
+
+    two = []
+    arrive(mid_a)
+    sa[...] = mid[0, x] + ra_mid[0] + ra_mid[1] + ra_mid[2]
+    for k in (2, 1, 3):
+        two.append(
+            send(sa.at[:, :, lanes((y + k) % NY, 128)], r2a.at[k - 1], A_TWO + k - 1, ys[k - 1])
+        )
+    arrive(mid_b)
     for i in range(NX):
-        sb[i, 0:16] = mid[1, i, :, :, y_lane] + rb_mid[0, i] + rb_mid[1, i] + rb_mid[2, i]
-        at = pl.ds(5 * i, 5)
-        sb[i, 16:21] = io[pl.ds(20 + 5 * i, 5), :, y_lane] + rb_io[0, at] + rb_io[1, at] + rb_io[2, at]
-    for k in (2, 1, 3):
-        one = copy(sb.at[(x + k) % NX], r2b.at[k - 1], B_TWO + k - 1, xs[k - 1])
-        one.start()
-        second.append(one)
-    for one in second:
-        one.wait_recv()
-    copies += second
+        sb[i] = mid[1, i, :, :, y_lane] + rb_mid[0, i] + rb_mid[1, i] + rb_mid[2, i]
+    for k in (2, 1, 3):
+        two.append(send(sb.at[(x + k) % NX], r2b.at[k - 1], B_TWO + k - 1, xs[k - 1]))
+
+    arrive(across_io)
+    mine_io[...] = ((rzi_two[0] + rzi_two[1]) + rzi_two[2]) + rzi_two[3]
+    share = []
+    for k in (2, 1, 3):
+        share.append(send(mine_io, ri.at[spot_z], Z_ALL + k, near_z[k - 1]))
+    ri[spot_z] = mine_io[...]
+
+    arrive(two)
     sum_a = sa[:, :, y_lane] + r2a[0] + r2a[1] + r2a[2]
     sum_b = sb[x] + r2b[0] + r2b[1] + r2b[2]
-
-    group, spot_z = z // 4, z % 4
-    io_tiles = [sum_a[16 + t] for t in range(5)] + [sum_b[16 + t] for t in range(5)]
-    io_tiles += [jnp.zeros((8, 128), F32)] * 2
     for i in range(4):
         for g in range(4):
             zs[i, g] = sum_a[4 * g + i]
             zs[i, 4 + g] = sum_b[4 * g + i]
-        for t in range(3):
-            zs[i, 8 + t] = io_tiles[4 * t + i]
     third = []
     for k in (2, 1, 3):
-        to = (spot_z + k) % 4
-        third.append(
-            copy(zs.at[to], rz.at[k - 1], Z_ONE + k, place(x, y, group * 4 + to, c))
-        )
-        third[-1].start()
-    for one in third:
-        one.wait_recv()
+        third.append(send(zs.at[(spot_z + k) % 4], rz.at[k - 1], Z_ONE + k, near_z[k - 1]))
+
+    arrive(share)
+    tile = lanes(c * NY + y, 128)
+    rows_a, rows_b = pl.ds(x * 5, 5), pl.ds((NX + x) * 5, 5)
+    for t in range(10):
+        full[(t // 5 * NX + x) * 5 + t % 5, :, tile] = ri[t % 4, t // 4]
+    gather = []
+    for k in (2, 1, 3):
+        spot = full.at[rows_a, :, tile]
+        gather.append(send(spot, spot, A_THREE + k - 1, ys[k - 1]))
+        spot = full.at[rows_b, :, tile]
+        gather.append(send(spot, spot, B_THREE + k - 1, xs[k - 1]))
+
+    arrive(third)
     grouped = zs[spot_z] + rz[0] + rz[1] + rz[2]
     for g in range(4):
         zs_two[g, 0] = grouped[g]
         zs_two[g, 1] = grouped[4 + g]
-        zs_two[g, 2:5] = grouped[8:11]
     across = []
     for k in (2, 1, 3):
-        to = (group + k) % 4
         across.append(
-            copy(zs_two.at[to], rz_two.at[group], Z_TWO + k, place(x, y, to * 4 + spot_z, c))
-        )
-        across[-1].start()
-    rz_two[group] = zs_two[group]
-    for one in across:
-        one.wait_recv()
-    copies += third + across
-    mine[...] = ((rz_two[0] + rz_two[1]) + rz_two[2]) + rz_two[3]
-
+            send(zs_two.at[(group + k) % 4], rz_two.at[k - 1], Z_TWO + k, far_z[k - 1])
+        )
+
+    arrive(gather)
+    fourth = []
+    for k in (2, 1, 3):
+        spot = full.at[rows_a, :, half]
+        fourth.append(send(spot, spot, A_FOUR + k - 1, xs[k - 1]))
+        spot = full.at[pl.ds(20, 20), :, tile]
+        fourth.append(send(spot, spot, B_FOUR + k - 1, ys[k - 1]))
+    arrive(fourth)
+    spot = full.at[:, :, half]
+    pair = send(spot, spot, PAIR, partner)
+
+    arrive(across)
+    mine[...] = zs_two[group] + rz_two[0] + rz_two[1] + rz_two[2]
     last = []
     for k in range(NY):
         if k:
-            one = copy(mine.at[c], r4.at[c, y], MID_ALL + k, ys[k - 1])
-            one.start()
-            last.append(one)
-        one = copy(
-            mine.at[1 - c], r4.at[c, y], MID_ALL + 4 + k, yo[k - 1] if k else partner
-        )
-        one.start()
-        last.append(one)
+            last.append(send(mine.at[c], r4.at[c, y], MID_ALL + k, ys[k - 1]))
+        last.append(
+            send(
+                mine.at[1 - c], r4.at[c, y], MID_ALL + 4 + k, yo[k - 1] if k else partner
+            )
+        )
     r4[c, y] = mine[c]
-    copies += last
-
-    share = []
-    for k in (2, 1, 3):
-        share.append(
-            copy(
-                mine.at[pl.ds(2, 3)], ri.at[spot_z], Z_ALL + k,
-                place(x, y, group * 4 + (spot_z + k) % 4, c),
-            )
-        )
-        share[-1].start()
-    ri[spot_z] = mine[2:5]
-    for one in share:
-        one.wait_recv()
-    copies += share
-    tile = lanes(c * NY + y, 128)
-    rows_a, rows_b = pl.ds(x * 5, 5), pl.ds((NX + x) * 5, 5)
-    for t in range(10):
-        full[(t // 5 * NX + x) * 5 + t % 5, :, tile] = ri[t % 4, t // 4]
-    third = []
-    for k in (2, 1, 3):
-        spot = full.at[rows_a, :, tile]
-        third.append(copy(spot, spot, A_THREE + k - 1, ys[k - 1]))
-        third[-1].start()
-        spot = full.at[rows_b, :, tile]
-        third.append(copy(spot, spot, B_THREE + k - 1, xs[k - 1]))
-        third[-1].start()
-    for one in third:
-        one.wait_recv()
-    fourth = []
-    for k in (2, 1, 3):
-        spot = full.at[rows_a, :, half]
-        fourth.append(copy(spot, spot, A_FOUR + k - 1, xs[k - 1]))
-        fourth[-1].start()
-        spot = full.at[pl.ds(20, 20), :, tile]
-        fourth.append(copy(spot, spot, B_FOUR + k - 1, ys[k - 1]))
-        fourth[-1].start()
-    for one in fourth:
-        one.wait_recv()
-    spot = full.at[:, :, half]
-    pair = copy(spot, spot, PAIR, partner)
-    pair.start()
-    for one in last:
-        one.wait_recv()
-    for i in range(8):
-        out_mid[:, pl.ds(128 * i, 128)] = r4[i // 4, i % 4]
-    copies += third + fourth + [pair]
     pair.wait_recv()
     out_in[...] = full[0:16].reshape(128, 1024)
     out_out[...] = full[16:40].reshape(192, 1024)[0:172]
+    arrive(last)
+    for i in range(8):
+        out_mid[:, pl.ds(128 * i, 128)] = r4[i // 4, i % 4]
 
     lax.fori_loop(1, NZ, pz_sent, 0)
     lax.fori_loop(1, NZ, zx_sent, 0)
@@ -468,12 +474,11 @@
             jax.ShapeDtypeStruct((8, 1024), F32),
             jax.ShapeDtypeStruct((172, 1024), F32),
         ),
-        in_specs=[hbm] * 10,
+        in_specs=[pl.BlockSpec(memory_space=pltpu.SMEM)] + [hbm] * 9,
         out_specs=(vmem,) * 4,
         scratch_shapes=[
             pltpu.SMEM((40,), jnp.int32),
             pltpu.SMEM((40,), jnp.int32),
-            pltpu.SMEM((1,), jnp.int32),
             buf((32, 512), F32),
             buf((40, 128, 128), BF16),
             buf((4, 128), jnp.int32),
@@ -514,26 +519,36 @@
             buf((3, 5, 8, 512), F32),
             buf((3, NX, NZ, 8, 128), F32),
             buf((3, 20, 8, 128), F32),
-            buf((21, 8, 512), F32),
-            buf((NX, 21, 8, 128), F32),
-            buf((3, 21, 8, 128), F32),
-            buf((3, 21, 8, 128), F32),
-            buf((4, 11, 8, 128), F32),
-            buf((3, 11, 8, 128), F32),
-            buf((4, 5, 8, 128), F32),
-            buf((4, 5, 8, 128), F32),
-            buf((5, 8, 128), F32),
+            buf((NZ, 8, 512), F32),
+            buf((NX, NZ, 8, 128), F32),
+            buf((3, NZ, 8, 128), F32),
+            buf((3, NZ, 8, 128), F32),
+            buf((4, 8, 8, 128), F32),
+            buf((3, 8, 8, 128), F32),
+            buf((4, 2, 8, 128), F32),
+            buf((3, 2, 8, 128), F32),
+            buf((2, 8, 128), F32),
             buf((4, 3, 8, 128), F32),
             buf((2, NY, 8, 128), F32),
             buf((40, 8, 1024), F32),
+            buf((5, 8, 512), F32),
+            buf((20, 8, 128), F32),
+            buf((3, 5, 8, 128), F32),
+            buf((3, 5, 8, 128), F32),
+            buf((4, 3, 8, 128), F32),
+            buf((3, 3, 8, 128), F32),
+            buf((4, 3, 8, 128), F32),
+            buf((3, 8, 128), F32),
             pltpu.SemaphoreType.DMA((SEMS,)),
             pltpu.SemaphoreType.DMA((SEMS,)),
-            pltpu.SemaphoreType.DMA((10,)),
+            pltpu.SemaphoreType.DMA((9,)),
         ],
         compiler_params=pltpu.CompilerParams(
-            collective_id=0, has_side_effects=True, vmem_limit_bytes=60 * 1024 * 1024
+            collective_id=0, has_side_effects=True, vmem_limit_bytes=46 * 1024 * 1024
         ),
-    )(tile_row, tile_col, tile_count, features, tiles, dest, cotangent, w_in, w_mid, w_out)
+    )(tile_count, *(pltpu.with_memory_space_constraint(v, pltpu.HBM) for v in (
+        tile_row, tile_col, features, tiles, dest, cotangent, w_in, w_mid, w_out
+    )))
 
 
 def shards(

time: 113 us -> 103 us (0.912)
  Pallas kernels: 105 us -> 99 us
  local copies, waits for them, and re-layouts: 6.77 us -> 2.9 us
    pallas_call x1, Pallas kernels: 105 us -> 99 us  [train(): pl.pallas_call(train_kernel, out_shape=(jax.ShapeDtypeStruct((128, 128),...]
    unnamed x4, local copies, waits for them, and re-layouts: 6.77 us -> 2.9 us
where the time goes in v2:
time: 103 us
  Pallas kernels  99 us (96%)
  local copies, waits for them, and re-layouts  2.9 us (3%)
  between operations  1.29 us (1%)
    pallas_call x1, Pallas kernels, train(): pl.pallas_call(train_kernel, out_shape=(jax.ShapeDtypeStruct((128, 128),...  99 us
    unnamed x4, local copies, waits for them, and re-layouts  2.9 us

profile of v2, /device:TPU:1, one launch (start us, length us, event | category | flops | bytes accessed | tf_op | source)
XLA Modules:
  0.0 103.2 jit_solution(10216672283567720421)
XLA Ops:
  1.3 99.0 %shard_map.129 = (f32[128,128]{1,0:T(8,128)S(1)}, f32[128,1024]{1,0:T(8,128)S(1)}, f32[8,1024]{1,0:T(8,128)S(1)}, f32[172,1024]{1,0:T(8,128)S(1)}) custom-call(s32[1]{0:T(128)S(6)} %copy.18.count_ref, s32[40]{0:T(128)} %row_hbm.1, s32[40]{0:T(128)} %col_hbm.1, f32[32,512]{1,0:T(8,128)} %feat_hbm.1, bf16[40,128,128]{2,1,0:T(8,128)(2,1)} %tiles_hbm.1, ...), custom_call_target="tpu_custom_call" | custom-call | tf_op jit(solution)/shard_map/pallas_call | solution.py:469
  100.3 0.6 copy.19
  100.9 0.8 copy.20
  101.7 0.6 copy.21
  102.3 0.9 copy.22

commit v3 on v2

--- a/solution.py
+++ b/solution.py
@@ -17,7 +17,7 @@
 
 
 EX_X, EX_C, EX_B = 0, 1, 2
-A_MID, A_IO, B_MID, B_IO = 3, 6, 9, 12
+A_IO, B_IO = 6, 12
 A_TWO, B_TWO = 15, 18
 Z_ONE, Z_TWO, Z_ALL = 21, 25, 29
 MID_ALL = 53
@@ -26,7 +26,8 @@
 REP_X, Z_X, XC_X = 78, 82, 98
 Z_P, XC_P = 106, 122
 A_TWO_IO, B_TWO_IO, Z_ONE_IO, Z_TWO_IO = 130, 133, 136, 140
-SEMS = 144
+MID_ONE = 144
+SEMS = 154
 
 
 def sigmoid(v):
@@ -323,15 +324,24 @@
         ).reshape(NZ, 2, 8, 512)
         mid[0, to] = rows[:, 0]
         mid[1, to] = rows[:, 1]
-        if k:
-            mid_a.append(send(mid.at[0, to], ra_mid.at[k - 1], A_MID + k - 1, xs[k - 1]))
-    for k in (2, 1, 3):
+
+    def send_mid(k, part, slot):
+        rows = pl.ds(*part)
+        mid_a.append(
+            send(
+                mid.at[0, (x + k) % NX, rows], ra_mid.at[k - 1, rows], slot, xs[k - 1]
+            )
+        )
+        blocks = pl.ds(part[0] // 4, part[1] // 4)
         mid_b.append(
             send(
-                mid.at[1, :, :, :, lanes((y + k) % NY, 128)],
-                rb_mid.at[k - 1], B_MID + k - 1, ys[k - 1],
+                mid.at[1, blocks, :, :, lanes((y + k) % NY, 128)],
+                rb_mid.at[k - 1, blocks], slot + 1, ys[k - 1],
             )
         )
+
+    send_mid(1, (0, 8), MID_ONE)
+    send_mid(3, (0, 8), MID_ONE + 2)
 
     y_lane = lanes(y, 128)
     two_io = []
@@ -347,6 +357,9 @@
         two_io.append(
             send(sbi.at[pl.ds((x + k) % NX * 5, 5)], r2bi.at[k - 1], B_TWO_IO + k - 1, xs[k - 1])
         )
+    send_mid(2, (0, 16), MID_ONE + 4)
+    send_mid(1, (8, 8), MID_ONE + 6)
+    send_mid(3, (8, 8), MID_ONE + 8)
     arrive(two_io)
     io_a = sai[:, :, y_lane] + r2ai[0] + r2ai[1] + r2ai[2]
     io_b = sbi[pl.ds(x * 5, 5)] + r2bi[0] + r2bi[1] + r2bi[2]
@@ -460,6 +473,16 @@
     lax.fori_loop(1, NZ, zx_sent, 0)
     for one in copies:
         one.wait_send()
+
+
+def write_kernel(*refs):
+    writes = [
+        pltpu.make_async_copy(refs[i], refs[4 + i], refs[8].at[i]) for i in range(4)
+    ]
+    for one in writes:
+        one.start()
+    for one in writes:
+        one.wait()
 
 
 def train(tile_row, tile_col, tile_count, features, tiles, dest, cotangent, w_in, w_mid, w_out):
@@ -555,9 +578,16 @@
     features, tiles, tile_row, tile_col, tile_count, dest_slot, w_in, w_mid, w_out, cotangent
 ):
     dest = dest_slot.reshape(4, 128)
-    return train(
+    results = train(
         tile_row, tile_col, tile_count, features, tiles, dest, cotangent, w_in, w_mid, w_out
     )
+    return pl.pallas_call(
+        write_kernel,
+        out_shape=tuple(jax.ShapeDtypeStruct(v.shape, v.dtype) for v in results),
+        in_specs=[pl.BlockSpec(memory_space=pltpu.VMEM)] * 4,
+        out_specs=(pl.BlockSpec(memory_space=pltpu.HBM),) * 4,
+        scratch_shapes=[pltpu.SemaphoreType.DMA((4,))],
+    )(*(pltpu.with_memory_space_constraint(v, pltpu.VMEM) for v in results))
 
 
 def solution(mesh):

time: 103 us -> 98 us (0.951)
  local copies, waits for them, and re-layouts: 2.9 us -> 0 us
  Pallas kernels: 99 us -> 96.5 us
    pallas_call x1, Pallas kernels: 99 us -> 95.4 us  [train(): pl.pallas_call(train_kernel, out_shape=(jax.ShapeDtypeStruct((128, 128),...]
    unnamed x4 -> x0, local copies, waits for them, and re-layouts: 2.9 us -> none
    pallas_call x0 -> x1, Pallas kernels: none -> 1.1 us  [shards(): pl.pallas_call(write_kernel, out_shape=tuple((jax.ShapeDtypeStruct(v.shap...]
where the time goes in v3:
time: 98 us; the launch traced here: 97.8 us
  Pallas kernels  96.5 us (98%)
  between operations  1.29 us (1%)
    pallas_call x1, Pallas kernels, train(): pl.pallas_call(train_kernel, out_shape=(jax.ShapeDtypeStruct((128, 128),...  95.4 us

profile of v3, /device:TPU:1, one launch (start us, length us, event | category | flops | bytes accessed | tf_op | source)
XLA Modules:
  0.0 97.8 jit_solution(3877494860490765386)
XLA Ops:
  1.3 95.4 %shard_map.129 = (f32[128,128]{1,0:T(8,128)S(1)}, f32[128,1024]{1,0:T(8,128)S(1)}, f32[8,1024]{1,0:T(8,128)S(1)}, f32[172,1024]{1,0:T(8,128)S(1)}) custom-call(s32[1]{0:T(128)S(6)} %copy.14.count_ref, s32[40]{0:T(128)} %row_hbm.1, s32[40]{0:T(128)} %col_hbm.1, f32[32,512]{1,0:T(8,128)} %feat_hbm.1, bf16[40,128,128]{2,1,0:T(8,128)(2,1)} %tiles_hbm.1, ...), custom_call_target="tpu_custom_call" | custom-call | tf_op jit(solution)/shard_map/pallas_call | solution.py:492
  96.7 1.1 %shard_map.130 = (f32[128,128]{1,0:T(8,128)}, f32[128,1024]{1,0:T(8,128)}, f32[8,1024]{1,0:T(8,128)}, f32[172,1024]{1,0:T(8,128)}) custom-call(f32[128,128]{1,0:T(8,128)S(1)} %get-tuple-element.8.refs_0_, f32[128,1024]{1,0:T(8,128)S(1)} %get-tuple-element.9.refs_1_, f32[8,1024]{1,0:T(8,128)S(1)} %get-tuple-element.10.refs_2_, ...), custom_call_target="tpu_custom_call" | custom-call | tf_op jit(solution)/shard_map/pallas_call | solution.py:584

commit v4 on v3

--- a/solution.py
+++ b/solution.py
@@ -163,7 +163,7 @@
         return made
 
     pz_start, pz_recv, pz_sent = over_z(p2, pz2, Z_P)
-    lax.fori_loop(1, NZ, pz_start, 0)
+    lax.fori_loop(1, NZ, pz_start, 0, unroll=True)
     pz2[z] = p2[z]
     wo[...] = jnp.zeros((192, 1024), BF16)
     for one in loads[3:]:
@@ -234,9 +234,9 @@
         one.wait_recv()
     t2[...] = rf[...].reshape(128, 128).T.reshape(NZ, 8, 128)
     zx_start, zx_recv, zx_sent = over_z(t2, rz2, Z_X)
-    lax.fori_loop(1, NZ, zx_start, 0)
+    lax.fori_loop(1, NZ, zx_start, 0, unroll=True)
     rz2[z] = t2[z]
-    lax.fori_loop(1, NZ, zx_recv, 0)
+    lax.fori_loop(1, NZ, zx_recv, 0, unroll=True)
     for i in range(8):
         rx[i] = rz2[:, i, :]
     xc_x = over_xc(rx, rq, XC_X)
@@ -278,7 +278,44 @@
     ex_b = copy(send_b, recv_b, EX_B, partner)
     ex_b.start()
 
+    def send(src, dst, slot, dev):
+        one = copy(src, dst, slot, dev)
+        one.start()
+        copies.append(one)
+        return one
+
+    def arrive(made):
+        for one in made:
+            one.wait_recv()
+
     copies += [ex_x, ex_b]
+    mid_a, mid_b = [], []
+    for k in (2, 1, 3, 0):
+        to = (x + k) % NX
+        rows = lax.dot_general(
+            h1[:, lanes(to, 256)], d2[...], LEADING, preferred_element_type=F32
+        ).reshape(NZ, 2, 8, 512)
+        mid[0, to] = rows[:, 0]
+        mid[1, to] = rows[:, 1]
+
+    def send_mid(k, part, slot):
+        rows = pl.ds(*part)
+        mid_a.append(
+            send(
+                mid.at[0, (x + k) % NX, rows], ra_mid.at[k - 1, rows], slot, xs[k - 1]
+            )
+        )
+        blocks = pl.ds(part[0] // 4, part[1] // 4)
+        mid_b.append(
+            send(
+                mid.at[1, blocks, :, :, lanes((y + k) % NY, 128)],
+                rb_mid.at[k - 1, blocks], slot + 1, ys[k - 1],
+            )
+        )
+
+    send_mid(1, (0, 8), MID_ONE)
+    send_mid(3, (0, 8), MID_ONE + 2)
+
     cot_rows = [cot2[i].astype(BF16) for i in range(2)]
     grad_out = jnp.dot(
         jnp.concatenate(cot_rows, axis=1), h2, preferred_element_type=F32
@@ -294,16 +331,6 @@
     grad_in = jnp.dot(x_rows, delta_one, preferred_element_type=F32).reshape(16, 8, 512)
     io[0:16] = grad_in
 
-    def send(src, dst, slot, dev):
-        one = copy(src, dst, slot, dev)
-        one.start()
-        copies.append(one)
-        return one
-
-    def arrive(made):
-        for one in made:
-            one.wait_recv()
-
     first_a, first_b = [], []
     for k in (2, 1, 3):
         first_a.append(
@@ -315,33 +342,8 @@
                 rb_io.at[k - 1], B_IO + k - 1, ys[k - 1],
             )
         )
-
-    mid_a, mid_b = [], []
-    for k in (2, 1, 3, 0):
-        to = (x + k) % NX
-        rows = lax.dot_general(
-            h1[:, lanes(to, 256)], d2[...], LEADING, preferred_element_type=F32
-        ).reshape(NZ, 2, 8, 512)
-        mid[0, to] = rows[:, 0]
-        mid[1, to] = rows[:, 1]
-
-    def send_mid(k, part, slot):
-        rows = pl.ds(*part)
-        mid_a.append(
-            send(
-                mid.at[0, (x + k) % NX, rows], ra_mid.at[k - 1, rows], slot, xs[k - 1]
-            )
-        )
-        blocks = pl.ds(part[0] // 4, part[1] // 4)
-        mid_b.append(
-            send(
-                mid.at[1, blocks, :, :, lanes((y + k) % NY, 128)],
-                rb_mid.at[k - 1, blocks], slot + 1, ys[k - 1],
-            )
-        )
-
-    send_mid(1, (0, 8), MID_ONE)
-    send_mid(3, (0, 8), MID_ONE + 2)
+    send_mid(1, (8, 8), MID_ONE + 6)
+    send_mid(3, (8, 8), MID_ONE + 8)
 
     y_lane = lanes(y, 128)
     two_io = []
@@ -358,8 +360,6 @@
             send(sbi.at[pl.ds((x + k) % NX * 5, 5)], r2bi.at[k - 1], B_TWO_IO + k - 1, xs[k - 1])
         )
     send_mid(2, (0, 16), MID_ONE + 4)
-    send_mid(1, (8, 8), MID_ONE + 6)
-    send_mid(3, (8, 8), MID_ONE + 8)
     arrive(two_io)
     io_a = sai[:, :, y_lane] + r2ai[0] + r2ai[1] + r2ai[2]
     io_b = sbi[pl.ds(x * 5, 5)] + r2bi[0] + r2bi[1] + r2bi[2]

time: 98 us -> 94.7 us (0.966)
  Pallas kernels: 96.5 us -> 93.2 us
    pallas_call x1, Pallas kernels: 95.4 us -> 92.1 us  [train(): pl.pallas_call(train_kernel, out_shape=(jax.ShapeDtypeStruct((128, 128),...]
where the time goes in v4:
time: 94.7 us; the launch traced here: 94.5 us
  Pallas kernels  93.2 us (98%)
  between operations  1.29 us (1%)
    pallas_call x1, Pallas kernels, train(): pl.pallas_call(train_kernel, out_shape=(jax.ShapeDtypeStruct((128, 128),...  92.1 us

profile of v4, /device:TPU:1, one launch (start us, length us, event | category | flops | bytes accessed | tf_op | source)
XLA Modules:
  0.0 94.5 jit_solution(10423232561678218608)
XLA Ops:
  1.3 92.1 %shard_map.129 = (f32[128,128]{1,0:T(8,128)S(1)}, f32[128,1024]{1,0:T(8,128)S(1)}, f32[8,1024]{1,0:T(8,128)S(1)}, f32[172,1024]{1,0:T(8,128)S(1)}) custom-call(s32[1]{0:T(128)S(6)} %copy.14.count_ref, s32[40]{0:T(128)} %row_hbm.1, s32[40]{0:T(128)} %col_hbm.1, f32[32,512]{1,0:T(8,128)} %feat_hbm.1, bf16[40,128,128]{2,1,0:T(8,128)(2,1)} %tiles_hbm.1, ...), custom_call_target="tpu_custom_call" | custom-call | tf_op jit(solution)/shard_map/pallas_call | solution.py:492
  93.4 1.1 %shard_map.130 = (f32[128,128]{1,0:T(8,128)}, f32[128,1024]{1,0:T(8,128)}, f32[8,1024]{1,0:T(8,128)}, f32[172,1024]{1,0:T(8,128)}) custom-call(f32[128,128]{1,0:T(8,128)S(1)} %get-tuple-element.8.refs_0_, f32[128,1024]{1,0:T(8,128)S(1)} %get-tuple-element.9.refs_1_, f32[8,1024]{1,0:T(8,128)S(1)} %get-tuple-element.10.refs_2_, ...), custom_call_target="tpu_custom_call" | custom-call | tf_op jit(solution)/shard_map/pallas_call | solution.py:584

commit v5 on v4

--- a/solution.py
+++ b/solution.py
@@ -50,7 +50,7 @@
     x2, cot2, xt, ct, wo, h1, slope1, d2, send_b, recv_b,
     mid, io, ra_mid, ra_io, rb_mid, rb_io, sa, sb, r2a, r2b, zs, rz, zs_two, rz_two, mine, ri, r4, full,
     sai, sbi, r2ai, r2bi, zi, rzi, rzi_two, mine_io,
-    ssem, rsem, lsem,
+    ssem, rsem, lsem, relay,
 ):
     loads = []
     for i, (src, dst) in enumerate((
@@ -85,16 +85,16 @@
     ys = [place(x, (y + k) % NY, z, c) for k in range(1, NY)]
     yo = [place(x, (y + k) % NY, z, 1 - c) for k in range(1, NY)]
     barrier = pltpu.get_barrier_semaphore()
-    for dev in [partner, far] + xs + xo + ys + yo:
+    zs_at = lambda k: place(x, y, (z + k) % NZ, c)
+    greeted = [partner, far] + xs + xo + ys + yo + [zs_at(1), zs_at(NZ - 1)]
+    for dev in greeted:
         pl.semaphore_signal(barrier, inc=1, device_id=dev, device_id_type=MESH)
 
-    def greet(k, carry):
-        pl.semaphore_signal(
-            barrier, inc=1, device_id=place(x, y, (z + k) % NZ, c), device_id_type=MESH
-        )
-        return carry
-
-    lax.fori_loop(1, NZ, greet, 0)
+    def tell(turn):
+        for k in (1 << turn, NZ - (1 << turn)):
+            pl.semaphore_signal(
+                relay.at[turn], inc=1, device_id=zs_at(k), device_id_type=MESH
+            )
 
     for one in loads[:3]:
         one.wait()
@@ -116,7 +116,8 @@
     p2[...] = lax.dot_general(
         hot[lanes(y, 128), :], within[...], TRAILING, preferred_element_type=F32
     ).reshape(NZ, 8, 128)
-    pl.semaphore_wait(barrier, 2 + 3 + 3 + 3 + 3 + NZ - 1)
+    pl.semaphore_wait(barrier, len(greeted))
+    tell(0)
 
     def halo(field, slot):
         one = copy(field.at[pl.ds(4, 4)], field.at[pl.ds(8 * c, 4)], slot, partner)
@@ -162,23 +163,24 @@
             made[-1].start()
         return made
 
-    pz_start, pz_recv, pz_sent = over_z(p2, pz2, Z_P)
-    lax.fori_loop(1, NZ, pz_start, 0, unroll=True)
-    pz2[z] = p2[z]
     wo[...] = jnp.zeros((192, 1024), BF16)
     for one in loads[3:]:
         one.wait()
     wo[0:172, :] = w_out_ref[...]
+    pl.semaphore_wait(relay.at[0], 2)
+    tell(1)
 
     count = count_ref[0]
 
-    def spread(field, near, wide):
+    def spread(field, near, wide, then=None):
         near.wait_recv()
         for i, part in enumerate(split(field[pl.ds(8 * (1 - c), 4)])):
             parts[pl.ds(8 * (1 - c), 4), pl.ds(32 * i, 32)] = part
         wide.wait_recv()
         for i, part in enumerate(split(field[pl.ds(8 * c, 4)])):
             parts[pl.ds(8 * c, 4), pl.ds(32 * i, 32)] = part
+        if then is not None:
+            then()
 
         def slots(i, sums):
             for u in range(5):
@@ -203,13 +205,16 @@
     copies += [near, wide]
     for i, part in enumerate(split(first)):
         parts[4:8, pl.ds(32 * i, 32)] = part
-    lax.fori_loop(1, NZ, pz_recv, 0)
-    for i in range(8):
-        px[i] = pz2[:, i, :]
-    xc_p = over_xc(px, pq, XC_P)
-    pq[mine_xc] = px[mine_xc]
-    copies += xc_p
-    second = spread(ext_two, near, wide)
+    pl.semaphore_wait(relay.at[1], 2)
+    tell(2)
+    pz_start, pz_recv, pz_sent = over_z(p2, pz2, Z_P)
+
+    def positions():
+        pl.semaphore_wait(relay.at[2], 2)
+        lax.fori_loop(1, NZ, pz_start, 0, unroll=True)
+        pz2[z] = p2[z]
+
+    second = spread(ext_two, near, wide, positions)
     second = 2.0 * second - ext[4:8]
     diffused = series_zero * ext[4:8] + series_one * ext_two[4:8] + series_two * second
 
@@ -226,21 +231,27 @@
         rep_x.append(copy(amsg.at[to], rf.at[y], REP_X + k, ys[k - 1]))
         rep_x[-1].start()
     rf[y] = amsg[y]
-    for one in xc_p:
-        one.wait_recv()
-    at_lane = lax.broadcasted_iota(jnp.int32, (128, 128), 1).astype(F32)
-    put[...] = jnp.where(pq[...].reshape(128, 128) == at_lane, 1.0, 0.0).astype(BF16)
     for one in rep_x:
         one.wait_recv()
     t2[...] = rf[...].reshape(128, 128).T.reshape(NZ, 8, 128)
     zx_start, zx_recv, zx_sent = over_z(t2, rz2, Z_X)
     lax.fori_loop(1, NZ, zx_start, 0, unroll=True)
     rz2[z] = t2[z]
+    lax.fori_loop(1, NZ, pz_recv, 0)
+    for i in range(8):
+        px[i] = pz2[:, i, :]
+    xc_p = over_xc(px, pq, XC_P)
+    pq[mine_xc] = px[mine_xc]
+    copies += xc_p
     lax.fori_loop(1, NZ, zx_recv, 0, unroll=True)
     for i in range(8):
         rx[i] = rz2[:, i, :]
     xc_x = over_xc(rx, rq, XC_X)
     rq[mine_xc] = rx[mine_xc]
+    for one in xc_p:
+        one.wait_recv()
+    at_lane = lax.broadcasted_iota(jnp.int32, (128, 128), 1).astype(F32)
+    put[...] = jnp.where(pq[...].reshape(128, 128) == at_lane, 1.0, 0.0).astype(BF16)
     for one in xc_x:
         one.wait_recv()
     copies += rep_x + xc_x
@@ -255,16 +266,18 @@
     ex_c.wait_recv()
     for i in range(2):
         ct[pl.ds(128 * i, 128), :] = cot2[i].T.astype(BF16)
-    ex_x.wait_recv()
-    for i in range(2):
-        xt[pl.ds(128 * i, 128), :] = x2[i].T.astype(BF16)
-
-    for j in range(4):
-        cols = pl.ds(256 * j, 256)
-        pre = jnp.dot(xt[...], w_in_ref[:, cols], preferred_element_type=F32)
-        g = sigmoid(pre)
-        h1[:, cols] = (pre * g).astype(BF16)
-        slope1[j] = g * (1.0 + pre * (1.0 - g))
+
+    for side in (c, 1 - c):
+        rows = lanes(side, 128)
+        if side is not c:
+            ex_x.wait_recv()
+        xt[rows, :] = x2[side].T.astype(BF16)
+        for j in range(4):
+            cols = pl.ds(256 * j, 256)
+            pre = jnp.dot(xt[rows, :], w_in_ref[:, cols], preferred_element_type=F32)
+            g = sigmoid(pre)
+            h1[rows, cols] = (pre * g).astype(BF16)
+            slope1[j, rows] = g * (1.0 + pre * (1.0 - g))
     half = lanes(c, 512)
     pre_two = jnp.dot(h1[...], w_mid_ref[:, half], preferred_element_type=F32)
     g_two = sigmoid(pre_two)
@@ -565,6 +578,7 @@
             pltpu.SemaphoreType.DMA((SEMS,)),
             pltpu.SemaphoreType.DMA((SEMS,)),
             pltpu.SemaphoreType.DMA((9,)),
+            pltpu.SemaphoreType.REGULAR((3,)),
         ],
         compiler_params=pltpu.CompilerParams(
             collective_id=0, has_side_effects=True, vmem_limit_bytes=46 * 1024 * 1024

time: 94.7 us -> 91.9 us (0.970)
  Pallas kernels: 93.2 us -> 90.5 us
    pallas_call x1, Pallas kernels: 92.1 us -> 89.4 us  [train(): pl.pallas_call(train_kernel, out_shape=(jax.ShapeDtypeStruct((128, 128),...]
where the time goes in v5:
time: 91.9 us; the launch traced here: 91.8 us
  Pallas kernels  90.5 us (98%)
  between operations  1.29 us (1%)
    pallas_call x1, Pallas kernels, train(): pl.pallas_call(train_kernel, out_shape=(jax.ShapeDtypeStruct((128, 128),...  89.4 us

profile of v5, /device:TPU:1, one launch (start us, length us, event | category | flops | bytes accessed | tf_op | source)
XLA Modules:
  0.0 91.8 jit_solution(14235837207680982348)
XLA Ops:
  1.3 89.4 %shard_map.129 = (f32[128,128]{1,0:T(8,128)S(1)}, f32[128,1024]{1,0:T(8,128)S(1)}, f32[8,1024]{1,0:T(8,128)S(1)}, f32[172,1024]{1,0:T(8,128)S(1)}) custom-call(s32[1]{0:T(128)S(6)} %copy.14.count_ref, s32[40]{0:T(128)} %row_hbm.1, s32[40]{0:T(128)} %col_hbm.1, f32[32,512]{1,0:T(8,128)} %feat_hbm.1, bf16[40,128,128]{2,1,0:T(8,128)(2,1)} %tiles_hbm.1, ...), custom_call_target="tpu_custom_call" | custom-call | tf_op jit(solution)/shard_map/pallas_call | solution.py:505
  90.7 1.1 %shard_map.130 = (f32[128,128]{1,0:T(8,128)}, f32[128,1024]{1,0:T(8,128)}, f32[8,1024]{1,0:T(8,128)}, f32[172,1024]{1,0:T(8,128)}) custom-call(f32[128,128]{1,0:T(8,128)S(1)} %get-tuple-element.8.refs_0_, f32[128,1024]{1,0:T(8,128)S(1)} %get-tuple-element.9.refs_1_, f32[8,1024]{1,0:T(8,128)S(1)} %get-tuple-element.10.refs_2_, ...), custom_call_target="tpu_custom_call" | custom-call | tf_op jit(solution)/shard_map/pallas_call | solution.py:598

commit v6 on v5

--- a/solution.py
+++ b/solution.py
@@ -52,14 +52,6 @@
     sai, sbi, r2ai, r2bi, zi, rzi, rzi_two, mine_io,
     ssem, rsem, lsem, relay,
 ):
-    loads = []
-    for i, (src, dst) in enumerate((
-        (feat_hbm, feat), (dest_hbm, dest), (cot_hbm, cot), (row_hbm, row_ref),
-        (col_hbm, col_ref), (tiles_hbm, tiles),
-        (w_in_hbm, w_in_ref), (w_out_hbm, w_out_ref), (w_mid_hbm, w_mid_ref),
-    )):
-        loads.append(pltpu.make_async_copy(src, dst, lsem.at[i]))
-        loads[-1].start()
     d = lax.axis_index("dom")
     y = lax.axis_index("rep")
     c = d % 2
@@ -96,14 +88,39 @@
                 relay.at[turn], inc=1, device_id=zs_at(k), device_id_type=MESH
             )
 
+    loads = []
+    for i, (src, dst) in enumerate((
+        (feat_hbm, feat), (dest_hbm, dest), (cot_hbm, cot), (row_hbm, row_ref),
+        (col_hbm, col_ref), (tiles_hbm, tiles),
+        (w_in_hbm, w_in_ref), (w_out_hbm, w_out_ref), (w_mid_hbm, w_mid_ref),
+    )):
+        loads.append(pltpu.make_async_copy(src, dst, lsem.at[i]))
+        loads[-1].start()
+    pl.semaphore_wait(barrier, len(greeted))
+
+    def halo(src, field, slot):
+        one = copy(src, field.at[2 * c], slot, partner)
+        two = copy(src, field.at[2 * (1 - c)], slot + 1, far)
+        two.start()
+        one.start()
+        return one, two
+
+    def keep_parts(value, slot):
+        for i, part in enumerate(split(value)):
+            for b in range(4):
+                parts[slot * 4 + b, pl.ds(32 * i, 32)] = part[:, 128 * b : 128 * b + 128]
+
+    near, wide = halo(feat_hbm, ext, HALO_ONE)
+    tell(0)
     for one in loads[:3]:
         one.wait()
-    own = jnp.stack([feat[:, pl.ds(128 * b, 128)] for b in range(4)])
-    ext[4:8] = own
-    for i, part in enumerate(split(own)):
-        parts[4:8, pl.ds(32 * i, 32)] = part
     cot2[c] = jnp.zeros((192, 128), F32)
     cot2[c, 0:172] = cot[...].astype(F32)
+    ex_c = copy(cot2.at[c], cot2.at[c], EX_C, partner)
+    ex_c.start()
+    copies = [near, wide, ex_c]
+    keep_parts(feat[...], 1)
+
     j = lax.broadcasted_iota(jnp.int32, (512, 128), 0)
     target = ((((j >> 1) & 3) * NZ + ((j >> 3) & 15)) * 2 + (j & 1)) * NY + (j >> 7)
     for b in range(4):
@@ -116,20 +133,8 @@
     p2[...] = lax.dot_general(
         hot[lanes(y, 128), :], within[...], TRAILING, preferred_element_type=F32
     ).reshape(NZ, 8, 128)
-    pl.semaphore_wait(barrier, len(greeted))
-    tell(0)
-
-    def halo(field, slot):
-        one = copy(field.at[pl.ds(4, 4)], field.at[pl.ds(8 * c, 4)], slot, partner)
-        two = copy(field.at[pl.ds(4, 4)], field.at[pl.ds(8 * (1 - c), 4)], slot + 1, far)
-        two.start()
-        one.start()
-        return one, two
-
-    near, wide = halo(ext, HALO_ONE)
-    ex_c = copy(cot2.at[c], cot2.at[c], EX_C, partner)
-    ex_c.start()
-    copies = [near, wide, ex_c]
+    pl.semaphore_wait(relay.at[0], 2)
+    tell(1)
     mine_xc = x * 2 + c
 
     def over_z(src, dst, slot):
@@ -167,18 +172,13 @@
     for one in loads[3:]:
         one.wait()
     wo[0:172, :] = w_out_ref[...]
-    pl.semaphore_wait(relay.at[0], 2)
-    tell(1)
-
     count = count_ref[0]
 
     def spread(field, near, wide, then=None):
         near.wait_recv()
-        for i, part in enumerate(split(field[pl.ds(8 * (1 - c), 4)])):
-            parts[pl.ds(8 * (1 - c), 4), pl.ds(32 * i, 32)] = part
+        keep_parts(field[2 * (1 - c)], 2 * (1 - c))
         wide.wait_recv()
-        for i, part in enumerate(split(field[pl.ds(8 * c, 4)])):
-            parts[pl.ds(8 * c, 4), pl.ds(32 * i, 32)] = part
+        keep_parts(field[2 * c], 2 * c)
         if then is not None:
             then()
 
@@ -197,14 +197,13 @@
             return sums
 
         zero = jnp.zeros((32, 128), F32)
-        return jnp.stack(lax.fori_loop(0, 8, slots, (zero,) * 4))
+        return jnp.concatenate(lax.fori_loop(0, 8, slots, (zero,) * 4), axis=1)
 
     first = spread(ext, near, wide)
-    ext_two[4:8] = first
-    near, wide = halo(ext_two, HALO_TWO)
+    ext_two[1] = first
+    near, wide = halo(ext_two.at[1], ext_two, HALO_TWO)
     copies += [near, wide]
-    for i, part in enumerate(split(first)):
-        parts[4:8, pl.ds(32 * i, 32)] = part
+    keep_parts(first, 1)
     pl.semaphore_wait(relay.at[1], 2)
     tell(2)
     pz_start, pz_recv, pz_sent = over_z(p2, pz2, Z_P)
@@ -215,12 +214,11 @@
         pz2[z] = p2[z]
 
     second = spread(ext_two, near, wide, positions)
-    second = 2.0 * second - ext[4:8]
-    diffused = series_zero * ext[4:8] + series_one * ext_two[4:8] + series_two * second
+    second = 2.0 * second - feat[...]
+    diffused = series_zero * feat[...] + series_one * ext_two[1] + series_two * second
 
     for i, part in enumerate(split(diffused)):
-        for b in range(4):
-            moved[pl.ds(32 * i, 32), pl.ds(128 * b, 128)] = part[b]
+        moved[pl.ds(32 * i, 32), :] = part
     sorted_rows = lax.dot_general(moved[...], hot[...], TRAILING, preferred_element_type=F32)
     columns = sorted_rows[0:32] + sorted_rows[32:64] + sorted_rows[64:96]
     for i in range(NY):
@@ -522,8 +520,8 @@
             buf((128, 1024), BF16),
             buf((1024, 1024), BF16),
             buf((172, 1024), BF16),
-            buf((12, 32, 128), F32),
-            buf((12, 32, 128), F32),
+            buf((3, 32, 512), F32),
+            buf((3, 32, 512), F32),
             buf((12, 96, 128), BF16),
             buf((512, 512), BF16),
             buf((96, 512), BF16),

time: 91.9 us -> 92.1 us (level)
  no operation moved by 1% of the time
where the time goes in v6:
time: 92.1 us; the launch traced here: 92 us
  Pallas kernels  90.7 us (98%)
  between operations  1.29 us (1%)
    pallas_call x1, Pallas kernels, train(): pl.pallas_call(train_kernel, out_shape=(jax.ShapeDtypeStruct((128, 128),...  89.6 us

profile of v6, /device:TPU:1, one launch (start us, length us, event | category | flops | bytes accessed | tf_op | source)
XLA Modules:
  0.0 92.0 jit_solution(5790131643544188478)
XLA Ops:
  1.3 89.6 %shard_map.129 = (f32[128,128]{1,0:T(8,128)S(1)}, f32[128,1024]{1,0:T(8,128)S(1)}, f32[8,1024]{1,0:T(8,128)S(1)}, f32[172,1024]{1,0:T(8,128)S(1)}) custom-call(s32[1]{0:T(128)S(6)} %copy.14.count_ref, s32[40]{0:T(128)} %row_hbm.1, s32[40]{0:T(128)} %col_hbm.1, f32[32,512]{1,0:T(8,128)} %feat_hbm.1, bf16[40,128,128]{2,1,0:T(8,128)(2,1)} %tiles_hbm.1, ...), custom_call_target="tpu_custom_call" | custom-call | tf_op jit(solution)/shard_map/pallas_call | solution.py:503
  90.9 1.1 %shard_map.130 = (f32[128,128]{1,0:T(8,128)}, f32[128,1024]{1,0:T(8,128)}, f32[8,1024]{1,0:T(8,128)}, f32[172,1024]{1,0:T(8,128)}) custom-call(f32[128,128]{1,0:T(8,128)S(1)} %get-tuple-element.8.refs_0_, f32[128,1024]{1,0:T(8,128)S(1)} %get-tuple-element.9.refs_1_, f32[8,1024]{1,0:T(8,128)S(1)} %get-tuple-element.10.refs_2_, ...), custom_call_target="tpu_custom_call" | custom-call | tf_op jit(solution)/shard_map/pallas_call | solution.py:596

commit v7 on v6

--- a/solution.py
+++ b/solution.py
@@ -174,13 +174,11 @@
     wo[0:172, :] = w_out_ref[...]
     count = count_ref[0]
 
-    def spread(field, near, wide, then=None):
+    def spread(field, near, wide):
         near.wait_recv()
         keep_parts(field[2 * (1 - c)], 2 * (1 - c))
         wide.wait_recv()
         keep_parts(field[2 * c], 2 * c)
-        if then is not None:
-            then()
 
         def slots(i, sums):
             for u in range(5):
@@ -207,13 +205,7 @@
     pl.semaphore_wait(relay.at[1], 2)
     tell(2)
     pz_start, pz_recv, pz_sent = over_z(p2, pz2, Z_P)
-
-    def positions():
-        pl.semaphore_wait(relay.at[2], 2)
-        lax.fori_loop(1, NZ, pz_start, 0, unroll=True)
-        pz2[z] = p2[z]
-
-    second = spread(ext_two, near, wide, positions)
+    second = spread(ext_two, near, wide)
     second = 2.0 * second - feat[...]
     diffused = series_zero * feat[...] + series_one * ext_two[1] + series_two * second
 
@@ -229,6 +221,9 @@
         rep_x.append(copy(amsg.at[to], rf.at[y], REP_X + k, ys[k - 1]))
         rep_x[-1].start()
     rf[y] = amsg[y]
+    pl.semaphore_wait(relay.at[2], 2)
+    lax.fori_loop(1, NZ, pz_start, 0, unroll=True)
+    pz2[z] = p2[z]
     for one in rep_x:
         one.wait_recv()
     t2[...] = rf[...].reshape(128, 128).T.reshape(NZ, 8, 128)
@@ -299,7 +294,11 @@
         for one in made:
             one.wait_recv()
 
-    copies += [ex_x, ex_b]
+    def drain(made):
+        for one in made:
+            one.wait_send()
+
+    early, copies = copies + [ex_x, ex_b], []
     mid_a, mid_b = [], []
     for k in (2, 1, 3, 0):
         to = (x + k) % NX
@@ -371,6 +370,9 @@
             send(sbi.at[pl.ds((x + k) % NX * 5, 5)], r2bi.at[k - 1], B_TWO_IO + k - 1, xs[k - 1])
         )
     send_mid(2, (0, 16), MID_ONE + 4)
+    drain(early)
+    lax.fori_loop(1, NZ, pz_sent, 0)
+    lax.fori_loop(1, NZ, zx_sent, 0)
     arrive(two_io)
     io_a = sai[:, :, y_lane] + r2ai[0] + r2ai[1] + r2ai[2]
     io_b = sbi[pl.ds(x * 5, 5)] + r2bi[0] + r2bi[1] + r2bi[2]
@@ -452,11 +454,13 @@
 
     arrive(gather)
     fourth = []
+    middle, copies = copies, []
     for k in (2, 1, 3):
         spot = full.at[rows_a, :, half]
         fourth.append(send(spot, spot, A_FOUR + k - 1, xs[k - 1]))
         spot = full.at[pl.ds(20, 20), :, tile]
         fourth.append(send(spot, spot, B_FOUR + k - 1, ys[k - 1]))
+    drain(middle)
     arrive(fourth)
     spot = full.at[:, :, half]
     pair = send(spot, spot, PAIR, partner)
@@ -480,10 +484,7 @@
     for i in range(8):
         out_mid[:, pl.ds(128 * i, 128)] = r4[i // 4, i % 4]
 
-    lax.fori_loop(1, NZ, pz_sent, 0)
-    lax.fori_loop(1, NZ, zx_sent, 0)
-    for one in copies:
-        one.wait_send()
+    drain(copies)
 
 
 def write_kernel(*refs):

time: 92.1 us -> 92.9 us (level)
  no operation moved by 1% of the time
where the time goes in v7:
time: 92.9 us; the launch traced here: 92.7 us
  Pallas kernels  91.4 us (98%)
  between operations  1.29 us (1%)
    pallas_call x1, Pallas kernels, train(): pl.pallas_call(train_kernel, out_shape=(jax.ShapeDtypeStruct((128, 128),...  90.3 us

profile of v7, /device:TPU:1, one launch (start us, length us, event | category | flops | bytes accessed | tf_op | source)
XLA Modules:
  0.0 92.7 jit_solution(15574855713982576645)
XLA Ops:
  1.3 90.3 %shard_map.129 = (f32[128,128]{1,0:T(8,128)S(1)}, f32[128,1024]{1,0:T(8,128)S(1)}, f32[8,1024]{1,0:T(8,128)S(1)}, f32[172,1024]{1,0:T(8,128)S(1)}) custom-call(s32[1]{0:T(128)S(6)} %copy.14.count_ref, s32[40]{0:T(128)} %row_hbm.1, s32[40]{0:T(128)} %col_hbm.1, f32[32,512]{1,0:T(8,128)} %feat_hbm.1, bf16[40,128,128]{2,1,0:T(8,128)(2,1)} %tiles_hbm.1, ...), custom_call_target="tpu_custom_call" | custom-call | tf_op jit(solution)/shard_map/pallas_call | solution.py:504
  91.6 1.1 %shard_map.130 = (f32[128,128]{1,0:T(8,128)}, f32[128,1024]{1,0:T(8,128)}, f32[8,1024]{1,0:T(8,128)}, f32[172,1024]{1,0:T(8,128)}) custom-call(f32[128,128]{1,0:T(8,128)S(1)} %get-tuple-element.8.refs_0_, f32[128,1024]{1,0:T(8,128)S(1)} %get-tuple-element.9.refs_1_, f32[8,1024]{1,0:T(8,128)S(1)} %get-tuple-element.10.refs_2_, ...), custom_call_target="tpu_custom_call" | custom-call | tf_op jit(solution)/shard_map/pallas_call | solution.py:597

commit v8 on v7

--- a/solution.py
+++ b/solution.py
@@ -174,9 +174,11 @@
     wo[0:172, :] = w_out_ref[...]
     count = count_ref[0]
 
-    def spread(field, near, wide):
+    def spread(field, near, wide, then=None):
         near.wait_recv()
         keep_parts(field[2 * (1 - c)], 2 * (1 - c))
+        if then is not None:
+            then()
         wide.wait_recv()
         keep_parts(field[2 * c], 2 * c)
 
@@ -205,7 +207,13 @@
     pl.semaphore_wait(relay.at[1], 2)
     tell(2)
     pz_start, pz_recv, pz_sent = over_z(p2, pz2, Z_P)
-    second = spread(ext_two, near, wide)
+
+    def positions():
+        pl.semaphore_wait(relay.at[2], 2)
+        lax.fori_loop(1, NZ, pz_start, 0, unroll=True)
+        pz2[z] = p2[z]
+
+    second = spread(ext_two, near, wide, positions)
     second = 2.0 * second - feat[...]
     diffused = series_zero * feat[...] + series_one * ext_two[1] + series_two * second
 
@@ -221,9 +229,6 @@
         rep_x.append(copy(amsg.at[to], rf.at[y], REP_X + k, ys[k - 1]))
         rep_x[-1].start()
     rf[y] = amsg[y]
-    pl.semaphore_wait(relay.at[2], 2)
-    lax.fori_loop(1, NZ, pz_start, 0, unroll=True)
-    pz2[z] = p2[z]
     for one in rep_x:
         one.wait_recv()
     t2[...] = rf[...].reshape(128, 128).T.reshape(NZ, 8, 128)

time: 92.9 us -> 91.8 us (0.988)
  Pallas kernels: 91.4 us -> 90.4 us
    pallas_call x1, Pallas kernels: 90.3 us -> 89.3 us  [train(): pl.pallas_call(train_kernel, out_shape=(jax.ShapeDtypeStruct((128, 128),...]
where the time goes in v8:
time: 91.8 us; the launch traced here: 91.7 us
  Pallas kernels  90.4 us (98%)
  between operations  1.29 us (1%)
    pallas_call x1, Pallas kernels, train(): pl.pallas_call(train_kernel, out_shape=(jax.ShapeDtypeStruct((128, 128),...  89.3 us

profile of v8, /device:TPU:1, one launch (start us, length us, event | category | flops | bytes accessed | tf_op | source)
XLA Modules:
  0.0 91.7 jit_solution(10831459663663888070)
XLA Ops:
  1.3 89.3 %shard_map.129 = (f32[128,128]{1,0:T(8,128)S(1)}, f32[128,1024]{1,0:T(8,128)S(1)}, f32[8,1024]{1,0:T(8,128)S(1)}, f32[172,1024]{1,0:T(8,128)S(1)}) custom-call(s32[1]{0:T(128)S(6)} %copy.14.count_ref, s32[40]{0:T(128)} %row_hbm.1, s32[40]{0:T(128)} %col_hbm.1, f32[32,512]{1,0:T(8,128)} %feat_hbm.1, bf16[40,128,128]{2,1,0:T(8,128)(2,1)} %tiles_hbm.1, ...), custom_call_target="tpu_custom_call" | custom-call | tf_op jit(solution)/shard_map/pallas_call | solution.py:509
  90.6 1.1 %shard_map.130 = (f32[128,128]{1,0:T(8,128)}, f32[128,1024]{1,0:T(8,128)}, f32[8,1024]{1,0:T(8,128)}, f32[172,1024]{1,0:T(8,128)}) custom-call(f32[128,128]{1,0:T(8,128)S(1)} %get-tuple-element.8.refs_0_, f32[128,1024]{1,0:T(8,128)S(1)} %get-tuple-element.9.refs_1_, f32[8,1024]{1,0:T(8,128)S(1)} %get-tuple-element.10.refs_2_, ...), custom_call_target="tpu_custom_call" | custom-call | tf_op jit(solution)/shard_map/pallas_call | solution.py:602

commit v9 on v5

--- a/solution.py
+++ b/solution.py
@@ -183,8 +183,8 @@
             then()
 
         def slots(i, sums):
-            for u in range(5):
-                s = i * 5 + u
+            for u in range(10):
+                s = i * 10 + u
                 at = jnp.minimum((col_ref[s] - 4 * d + 4) & 511, 11)
                 product = lax.dot_general(
                     parts[at], tiles[s], TRAILING, preferred_element_type=F32
@@ -197,7 +197,7 @@
             return sums
 
         zero = jnp.zeros((32, 128), F32)
-        return jnp.stack(lax.fori_loop(0, 8, slots, (zero,) * 4))
+        return jnp.stack(lax.fori_loop(0, 4, slots, (zero,) * 4))
 
     first = spread(ext, near, wide)
     ext_two[4:8] = first
@@ -326,8 +326,7 @@
             )
         )
 
-    send_mid(1, (0, 8), MID_ONE)
-    send_mid(3, (0, 8), MID_ONE + 2)
+    send_mid(2, (0, 8), MID_ONE)
 
     cot_rows = [cot2[i].astype(BF16) for i in range(2)]
     grad_out = jnp.dot(
@@ -355,8 +354,7 @@
                 rb_io.at[k - 1], B_IO + k - 1, ys[k - 1],
             )
         )
-    send_mid(1, (8, 8), MID_ONE + 6)
-    send_mid(3, (8, 8), MID_ONE + 8)
+    send_mid(2, (8, 8), MID_ONE + 2)
 
     y_lane = lanes(y, 128)
     two_io = []
@@ -372,7 +370,8 @@
         two_io.append(
             send(sbi.at[pl.ds((x + k) % NX * 5, 5)], r2bi.at[k - 1], B_TWO_IO + k - 1, xs[k - 1])
         )
-    send_mid(2, (0, 16), MID_ONE + 4)
+    send_mid(1, (0, 16), MID_ONE + 4)
+    send_mid(3, (0, 16), MID_ONE + 6)
     arrive(two_io)
     io_a = sai[:, :, y_lane] + r2ai[0] + r2ai[1] + r2ai[2]
     io_b = sbi[pl.ds(x * 5, 5)] + r2bi[0] + r2bi[1] + r2bi[2]

time: 91.9 us -> 90 us (0.979)
  Pallas kernels: 90.5 us -> 88.6 us
    pallas_call x1, Pallas kernels: 89.4 us -> 87.5 us  [train(): pl.pallas_call(train_kernel, out_shape=(jax.ShapeDtypeStruct((128, 128),...]
where the time goes in v9:
time: 90 us; the launch traced here: 89.9 us
  Pallas kernels  88.6 us (98%)
  between operations  1.29 us (1%)
    pallas_call x1, Pallas kernels, train(): pl.pallas_call(train_kernel, out_shape=(jax.ShapeDtypeStruct((128, 128),...  87.5 us

profile of v9, /device:TPU:1, one launch (start us, length us, event | category | flops | bytes accessed | tf_op | source)
XLA Modules:
  0.0 89.9 jit_solution(17852008269213460618)
XLA Ops:
  1.3 87.5 %shard_map.129 = (f32[128,128]{1,0:T(8,128)S(1)}, f32[128,1024]{1,0:T(8,128)S(1)}, f32[8,1024]{1,0:T(8,128)S(1)}, f32[172,1024]{1,0:T(8,128)S(1)}) custom-call(s32[1]{0:T(128)S(6)} %copy.14.count_ref, s32[40]{0:T(128)} %row_hbm.1, s32[40]{0:T(128)} %col_hbm.1, f32[32,512]{1,0:T(8,128)} %feat_hbm.1, bf16[40,128,128]{2,1,0:T(8,128)(2,1)} %tiles_hbm.1, ...), custom_call_target="tpu_custom_call" | custom-call | tf_op jit(solution)/shard_map/pallas_call | solution.py:504
  88.8 1.1 %shard_map.130 = (f32[128,128]{1,0:T(8,128)}, f32[128,1024]{1,0:T(8,128)}, f32[8,1024]{1,0:T(8,128)}, f32[172,1024]{1,0:T(8,128)}) custom-call(f32[128,128]{1,0:T(8,128)S(1)} %get-tuple-element.8.refs_0_, f32[128,1024]{1,0:T(8,128)S(1)} %get-tuple-element.9.refs_1_, f32[8,1024]{1,0:T(8,128)S(1)} %get-tuple-element.10.refs_2_, ...), custom_call_target="tpu_custom_call" | custom-call | tf_op jit(solution)/shard_map/pallas_call | solution.py:597
